TPU v7x, 32 devices: a whole 2x2x4 slice. The times are simulated.
32 devices in a mesh: groups: 2 (over y), space: 8 (over z, x), batch: 2 (over core).
Axes of the slice: x: 2, y: 2, z: 4, core: 2. Of those that a mesh axis runs over, the one named last changes fastest.
Arguments:
- inputs: bfloat16 [4, 8, 8, 8, 8, 1024], P(('groups', 'batch'), 'space'), parts along dimension 0, may hold values from -6 to 6
- cotangent: bfloat16 [4, 8, 8, 8, 8, 1024], P(('groups', 'batch'), 'space'), parts along dimension 0, may hold values from -6 to 6
- offsets: int32 [4], P(('groups', 'batch')), parts along dimension 0, may hold values from 1 to 7
- w_qkv: bfloat16 [1024, 3072], P('batch'), may hold values from -0.375 to 0.375
- w_out: bfloat16 [1024, 1024], P('batch'), may hold values from -0.1875 to 0.1875
- gain: float32 [1024], replicated, may hold values from 0.5 to 2, as said below
Outputs:
- update: bfloat16 [4, 8, 8, 8, 8, 1024], P(('groups', 'batch'), 'space'), parts along dimension 0
- grad: bfloat16 [4, 8, 8, 8, 8, 1024], P(('groups', 'batch'), 'space'), parts along dimension 0
There are 2 independent parts, one for each index of `groups`. A program takes and returns all parts, laid end to end along the dimension named above; an argument that names none is the same for every part. Nothing has to cross between parts.
Inputs may be any that keep to these rules, and one draw needn't show every extreme that they name: `gain`: positive gains.
All inputs are finite; a program needn't handle non-finite values.
Results may differ from a plain program's by a relative error of at most 0.005.
The roundings to bfloat16 on the way count: a program that leaves them out, or rounds other values in their place, can miss the bound.
Values may be sent and summed in bfloat16 or wider, within the bound.
A program may use at most 128 MiB of HBM per device.

v0:
```python
import jax
import jax.numpy as jnp
from jax import lax
from jax.sharding import PartitionSpec as P

WIN = 8
YTILES = 4
HEAD_DIM = 64


EPS = 1e-05
GROUP_HEADS = 4


def passed_along(x, axis, by):
    size = lax.axis_size(axis)
    return lax.ppermute(x, axis, [(i, (i + by) % size) for i in range(size)])


def to_windows(grid_field):
    extent_x, extent_y, extent_z, channels = grid_field.shape
    window_side = WIN
    blocks = grid_field.reshape(
        extent_x // window_side,
        window_side,
        extent_y // window_side,
        window_side,
        extent_z // window_side,
        window_side,
        channels,
    )
    blocks = blocks.transpose(0, 2, 4, 1, 3, 5, 6)
    return blocks.reshape(-1, window_side * window_side * window_side, channels)


def from_windows(window_stack, extent_x, extent_y, extent_z):
    window_side = WIN
    channels = window_stack.shape[-1]
    blocks = window_stack.reshape(
        extent_x // window_side,
        extent_y // window_side,
        extent_z // window_side,
        window_side,
        window_side,
        window_side,
        channels,
    )
    blocks = blocks.transpose(0, 3, 1, 4, 2, 5, 6)
    return blocks.reshape(extent_x, extent_y, extent_z, channels)


def split_heads(matrix):
    row_count = matrix.shape[0]
    return matrix.reshape(row_count, -1, GROUP_HEADS, HEAD_DIM).transpose(1, 0, 2, 3)


def join_heads(grouped):
    return grouped.transpose(1, 0, 2, 3).reshape(grouped.shape[1], -1)


def group_scores(query, keys):
    return jnp.einsum(
        "qhd,khd->hqk", query, keys, preferred_element_type=jnp.float32
    ) * HEAD_DIM ** (-0.5)


def probabilities(scores):
    peak = jnp.max(scores, axis=-1, keepdims=True)
    raised = jnp.exp(scores - peak)
    return raised / jnp.sum(raised, axis=-1, keepdims=True)


def attend_group(operands):
    query, keys, values = operands
    soft_low = probabilities(group_scores(query, keys)).astype(jnp.bfloat16)
    return jnp.einsum("hqk,khd->qhd", soft_low, values, preferred_element_type=jnp.float32).astype(
        jnp.bfloat16
    )


def reverse_group(operands):
    query, keys, values, upstream = operands
    soft = probabilities(group_scores(query, keys))
    grad_weights = jnp.einsum("qhd,khd->hqk", upstream, values, preferred_element_type=jnp.float32)
    grad_scores = (
        soft
        * (grad_weights - jnp.sum(grad_weights * soft, axis=-1, keepdims=True))
        * HEAD_DIM ** (-0.5)
    ).astype(jnp.bfloat16)
    grad_query = jnp.einsum(
        "hqk,khd->qhd", grad_scores, keys, preferred_element_type=jnp.float32
    ).astype(jnp.bfloat16)
    grad_keys = jnp.einsum(
        "hqk,qhd->khd", grad_scores, query, preferred_element_type=jnp.float32
    ).astype(jnp.bfloat16)
    soft_low = soft.astype(jnp.bfloat16)
    grad_values = jnp.einsum(
        "hqk,qhd->khd", soft_low, upstream, preferred_element_type=jnp.float32
    ).astype(jnp.bfloat16)
    return (grad_query, grad_keys, grad_values)


def attend_window(operands):
    grouped = tuple((split_heads(member) for member in operands))
    return join_heads(lax.map(attend_group, grouped))


def reverse_window(operands):
    grouped = tuple((split_heads(member) for member in operands))
    grad_query, grad_keys, grad_values = lax.map(reverse_group, grouped)
    return jnp.concatenate(
        [join_heads(grad_query), join_heads(grad_keys), join_heads(grad_values)], axis=1
    )


def contract_rows(left, right):
    return lax.dot_general(
        left, right, (((1,), (1,)), ((), ())), preferred_element_type=jnp.float32
    )


def shards(inputs, cotangent, offsets, w_qkv, w_out, gain):
    tiled_shape = inputs.shape
    cand_count, tile_count, slab, slab_y, extent_z, channels = tiled_shape
    inputs = inputs.reshape(cand_count, slab, slab_y, extent_z, channels)
    cotangent = cotangent.reshape(cand_count, slab, slab_y, extent_z, channels)
    window_tokens = slab * slab * slab
    after_in, after_cot = passed_along((inputs, cotangent), "space", -YTILES)

    def enter(own, later, start):
        joined = jnp.concatenate([own, later], axis=0)
        return to_windows(lax.dynamic_slice_in_dim(joined, start, slab, 0))

    def leave(own, earlier, start):
        joined = jnp.concatenate([earlier, own], axis=0)
        return lax.dynamic_slice_in_dim(joined, slab - start, slab, 0)

    def to_frame(flat):
        stacked = flat.reshape(cand_count, -1, window_tokens, channels)

        def rebuild(window_stack):
            return from_windows(window_stack, slab, slab_y, extent_z)

        return jax.vmap(rebuild)(stacked)

    enter_all = jax.vmap(enter)
    leave_all = jax.vmap(leave)
    win_in = enter_all(inputs, after_in, offsets).reshape(-1, channels)
    win_cot = enter_all(cotangent, after_cot, offsets).reshape(-1, channels)
    values32 = win_in.astype(jnp.float32)
    center = values32 - jnp.mean(values32, axis=-1, keepdims=True)
    inverse = lax.rsqrt(jnp.mean(center * center, axis=-1, keepdims=True) + EPS)
    normed = center * inverse
    scaled = (normed * gain).astype(jnp.bfloat16)
    columns = scaled
    projected = jnp.dot(
        columns,
        lax.all_gather(w_qkv, "batch", axis=0, tiled=True),
        preferred_element_type=jnp.float32,
    )
    query = projected[:, :channels].astype(jnp.bfloat16).reshape(-1, window_tokens, channels)
    keys = (
        projected[:, channels : 2 * channels]
        .astype(jnp.bfloat16)
        .reshape(-1, window_tokens, channels)
    )
    values = projected[:, 2 * channels :].astype(jnp.bfloat16).reshape(-1, window_tokens, channels)
    attended = lax.map(attend_window, (query, keys, values)).reshape(-1, channels)
    columns = attended
    frame_update = jnp.dot(
        columns,
        lax.all_gather(w_out, "batch", axis=0, tiled=True),
        preferred_element_type=jnp.float32,
    )
    frame_update = to_frame(frame_update.astype(jnp.bfloat16))
    before_update = passed_along(frame_update, "space", YTILES)
    update = leave_all(frame_update, before_update, offsets)
    upstream = contract_rows(win_cot, lax.all_gather(w_out, "batch", axis=0, tiled=True))
    upstream = upstream.astype(jnp.bfloat16).reshape(-1, window_tokens, channels)
    grad_qkv = lax.map(reverse_window, (query, keys, values, upstream)).reshape(-1, 3 * channels)
    grad_back_proj = contract_rows(grad_qkv, lax.all_gather(w_qkv, "batch", axis=0, tiled=True))
    grad_normed = grad_back_proj * gain
    mean_grad = jnp.mean(grad_normed, axis=-1, keepdims=True)
    mean_mixed = jnp.mean(grad_normed * normed, axis=-1, keepdims=True)
    frame_grad = to_frame(
        (inverse * (grad_normed - mean_grad - normed * mean_mixed)).astype(jnp.bfloat16)
    )
    before_grad = passed_along(frame_grad, "space", YTILES)
    grad = leave_all(frame_grad, before_grad, offsets)
    return (update.reshape(tiled_shape), grad.reshape(tiled_shape))


def solution(mesh):
    in_specs = (
        P(("groups", "batch"), "space", None, None, None, None),
        P(("groups", "batch"), "space", None, None, None, None),
        P(("groups", "batch")),
        P("batch", None),
        P("batch", None),
        P(),
    )
    out_specs = (
        P(("groups", "batch"), "space", None, None, None, None),
        P(("groups", "batch"), "space", None, None, None, None),
    )
    return jax.shard_map(shards, mesh=mesh, in_specs=in_specs, out_specs=out_specs, check_vma=False)
```

profile of v0, /device:TPU:0, one launch (start us, length us, event | category | flops | bytes accessed | tf_op | source)
XLA Modules:
  0.0 379.8 jit_solution(6362064723904219643)
XLA Ops:
  8.7 4.1 %collective-permute-start = (bf16[1,8,8,8,1024]{4,3,2,1,0:T(8,128)(2,1)S(1)}, bf16[1,8,8,8,1024]{4,3,2,1,0:T(8,128)(2,1)S(1)}, u32[]{:S(2)}, u32[]{:S(2)}) collective-permute-start(bf16[1,8,8,8,1024]{4,3,2,1,0:T(8,128)(2,1)S(1)} %bitcast.174), channel_id=1, source_target_pairs={{0,8},{2,10},{4,12},{6,14},{8,0},{10,2},{12,4},{14,6},{1,9},{3,11}... | collective-permute-start | bytes 3145736 | tf_op jit(solution)/shard_map/ppermute | solution.py:17
  13.5 68.2 %collective-permute-done = bf16[1,8,8,8,1024]{4,3,2,1,0:T(8,128)(2,1)S(1)} collective-permute-done((bf16[1,8,8,8,1024]{4,3,2,1,0:T(8,128)(2,1)S(1)}, bf16[1,8,8,8,1024]{4,3,2,1,0:T(8,128)(2,1)S(1)}, u32[]{:S(2)}, u32[]{:S(2)}) %collective-permute-start) | collective-permute-done | bytes 1048608 | tf_op jit(solution)/shard_map/ppermute | solution.py:17
  82.7 1.4 convert_reduce_fusion
  84.7 18.7 %collective-permute-done.2 = bf16[1,8,8,8,1024]{4,3,2,1,0:T(8,128)(2,1)} collective-permute-done((bf16[1,8,8,8,1024]{4,3,2,1,0:T(8,128)(2,1)S(1)}, bf16[1,8,8,8,1024]{4,3,2,1,0:T(8,128)(2,1)}, u32[]{:S(2)}, u32[]{:S(2)}) %collective-permute-start.2) | collective-permute-done | bytes 1048608 | tf_op jit(solution)/shard_map/ppermute | solution.py:17
  103.5 1.3 fusion.138
  105.2 3.8 %convolution_convert_fusion.1 = bf16[512,1024]{1,0:T(8,128)(2,1)} fusion(bf16[512,1024]{1,0:T(8,128)(2,1)S(1)} %bitcast.183, bf16[1024,1024]{1,0:T(8,128)(2,1)} %all-gather.5.cloned.1.call-done), kind=kOutput, calls=%fused_computation.106 | convolution fusion | flops 1074266112 | bytes 4194304 | tf_op jit(solution)/shard_map/dot_general | solution.py:117
  109.0 1.5 copy.23
  110.6 6.4 %convolution_convert_fusion = bf16[512,3072]{1,0:T(8,128)(2,1)S(1)} fusion(bf16[512,1024]{1,0:T(8,128)(2,1)S(1)} %multiply_convert_fusion.2, bf16[1024,3072]{1,0:T(8,128)(2,1)} %all-gather.3.cloned.1.call-done), kind=kOutput, calls=%fused_computation.83 | convolution fusion | flops 3222798336 | bytes 10485760 | tf_op jit(solution)/shard_map/dot_general | solution.py:156
  117.0 1.7 fusion.162
  118.7 2.3 copy.22
  121.0 1.3 copy.21
  122.4 1.5 copy.20
  124.9 31.8 %while.44 = (s32[]{:T(128)}, bf16[4,512,4,64]{1,3,2,0:T(8,128)(2,1)}, bf16[4,512,4,64]{1,3,2,0:T(8,128)(2,1)S(1)}, bf16[4,512,4,64]{1,3,2,0:T(8,128)(2,1)}, bf16[4,512,4,64]{1,3,2,0:T(8,128)(2,1)}, /*index=5*/s32[]{:T(128)}) while((s32[]{:T(128)}, bf16[4,512,4,64]{1,3,2,0:T(8,128)(2,1)}, bf16[4,512,4,64]{1,3,2,0:T(8,128)(2,1)S(1)}, ...), condition=%wide.region_5.0_spmd, body=%wide.region_2.5_spmd.sunk | while | flops 273809920 | bytes 9455693 | solution.py:105
  124.9 4.6 %fusion.193 = (f32[4,512]{1,0:T(4,128)S(1)}, f32[4,512,512]{1,2,0:T(8,128)}) fusion(bf16[4,512,4,64]{1,3,2,0:T(8,128)(2,1)} %get-tuple-element.298, s32[]{:T(128)S(6)} %copy.34, bf16[4,512,4,64]{1,3,2,0:T(8,128)(2,1)} %get-tuple-element.297), kind=kOutput, calls=%fused_computation.119.clone.1 | convolution fusion | flops 137363968 | bytes 4727808 | tf_op jit(solution)/shard_map/while/body/eval_jaxpr/while/body/eval_jaxpr/sub | solution.py:69
  129.5 3.4 fusion.194
  132.9 4.6 %fusion.193 = (f32[4,512]{1,0:T(4,128)S(1)}, f32[4,512,512]{1,2,0:T(8,128)}) fusion(bf16[4,512,4,64]{1,3,2,0:T(8,128)(2,1)} %get-tuple-element.298, s32[]{:T(128)S(6)} %copy.34, bf16[4,512,4,64]{1,3,2,0:T(8,128)(2,1)} %get-tuple-element.297), kind=kOutput, calls=%fused_computation.119.clone.1 | convolution fusion | flops 137363968 | bytes 4727808 | tf_op jit(solution)/shard_map/while/body/eval_jaxpr/while/body/eval_jaxpr/sub | solution.py:69
  137.5 3.4 fusion.194
  140.9 4.6 %fusion.193 = (f32[4,512]{1,0:T(4,128)S(1)}, f32[4,512,512]{1,2,0:T(8,128)}) fusion(bf16[4,512,4,64]{1,3,2,0:T(8,128)(2,1)} %get-tuple-element.298, s32[]{:T(128)S(6)} %copy.34, bf16[4,512,4,64]{1,3,2,0:T(8,128)(2,1)} %get-tuple-element.297), kind=kOutput, calls=%fused_computation.119.clone.1 | convolution fusion | flops 137363968 | bytes 4727808 | tf_op jit(solution)/shard_map/while/body/eval_jaxpr/while/body/eval_jaxpr/sub | solution.py:69
  145.4 3.4 fusion.194
  148.8 4.6 %fusion.193 = (f32[4,512]{1,0:T(4,128)S(1)}, f32[4,512,512]{1,2,0:T(8,128)}) fusion(bf16[4,512,4,64]{1,3,2,0:T(8,128)(2,1)} %get-tuple-element.298, s32[]{:T(128)S(6)} %copy.34, bf16[4,512,4,64]{1,3,2,0:T(8,128)(2,1)} %get-tuple-element.297), kind=kOutput, calls=%fused_computation.119.clone.1 | convolution fusion | flops 137363968 | bytes 4727808 | tf_op jit(solution)/shard_map/while/body/eval_jaxpr/while/body/eval_jaxpr/sub | solution.py:69
  153.4 3.4 fusion.194
  160.0 110.7 %while.45 = (s32[]{:T(128)}, bf16[4,512,4,64]{1,3,2,0:T(8,128)(2,1)}, bf16[4,512,4,64]{1,3,2,0:T(8,128)(2,1)}, bf16[4,512,4,64]{1,3,2,0:T(8,128)(2,1)}, bf16[4,5...) while((s32[]{:T(128)}, ...), condition=%wide.region_10.11_spmd, body=%wide.region_6.10_spmd.sunk | while | flops 691410432 | bytes 48813156 | solution.py:110
  160.0 2.8 fusion.205
  162.8 4.6 %fusion.206 = (f32[4,512]{1,0:T(4,128)S(1)}, f32[4,512,512]{1,2,0:T(8,128)}) fusion(bf16[4,512,4,64]{1,3,2,0:T(8,128)(2,1)} %get-tuple-element.323, s32[]{:T(128)S(6)} %copy.42, bf16[4,512,4,64]{1,3,2,0:T(8,128)(2,1)} %get-tuple-element.322), kind=kOutput, calls=%fused_computation.120.clone.1 | convolution fusion | flops 137363968 | bytes 4727808 | tf_op jit(solution)/shard_map/while/body/eval_jaxpr/while/body/eval_jaxpr/sub | solution.py:69
  167.4 3.7 fusion.209
  171.1 8.2 %fusion.208 = bf16[4,512,4,64]{1,3,2,0:T(8,128)(2,1)} fusion(bf16[4,512,4,64]{1,3,2,0:T(8,128)(2,1)} %get-tuple-element.311, s32[]{:T(128)S(6)} %copy.42, f32[4,512,512]{1,2,0:T(8,128)} %fusion.205, bf16[4,512,4,64]{1,3,2,0:T(8,128)(2,1)} %get-tuple-element.323, f32[4,512,512]{1,2,0:T(8,128)} %get-tuple-element.280, f32[4,512]{1,0:T(4,128)S(1)} %get-tuple-element.281), kind=kOutput, calls=%fused_computation.48.clone.1 | convolution fusion | flops 141691392 | bytes 17318912 | tf_op jit(solution)/shard_map/while/body/eval_jaxpr/while/body/eval_jaxpr/hqk,qhd->khd/dot_general | solution.py:93
  179.3 8.4 %fusion.207 = bf16[4,512,4,64]{1,3,2,0:T(8,128)(2,1)} fusion(bf16[4,512,4,64]{1,3,2,0:T(8,128)(2,1)} %get-tuple-element.310, s32[]{:T(128)S(6)} %copy.42, f32[4,512,512]{1,2,0:T(8,128)} %fusion.205, bf16[4,512,4,64]{1,3,2,0:T(8,128)(2,1)} %get-tuple-element.322, f32[4,512,512]{1,2,0:T(8,128)} %get-tuple-element.280, f32[4,512]{1,0:T(4,128)S(1)} %get-tuple-element.281), kind=kOutput, calls=%fused_computation.50.clone.1 | convolution fusion | flops 141691392 | bytes 17318912 | tf_op jit(solution)/shard_map/while/body/eval_jaxpr/while/body/eval_jaxpr/hqk,khd->qhd/dot_general | solution.py:90
  187.7 2.8 fusion.205
  190.5 4.6 %fusion.206 = (f32[4,512]{1,0:T(4,128)S(1)}, f32[4,512,512]{1,2,0:T(8,128)}) fusion(bf16[4,512,4,64]{1,3,2,0:T(8,128)(2,1)} %get-tuple-element.323, s32[]{:T(128)S(6)} %copy.42, bf16[4,512,4,64]{1,3,2,0:T(8,128)(2,1)} %get-tuple-element.322), kind=kOutput, calls=%fused_computation.120.clone.1 | convolution fusion | flops 137363968 | bytes 4727808 | tf_op jit(solution)/shard_map/while/body/eval_jaxpr/while/body/eval_jaxpr/sub | solution.py:69
  195.1 3.7 fusion.209
  198.8 8.1 %fusion.208 = bf16[4,512,4,64]{1,3,2,0:T(8,128)(2,1)} fusion(bf16[4,512,4,64]{1,3,2,0:T(8,128)(2,1)} %get-tuple-element.311, s32[]{:T(128)S(6)} %copy.42, f32[4,512,512]{1,2,0:T(8,128)} %fusion.205, bf16[4,512,4,64]{1,3,2,0:T(8,128)(2,1)} %get-tuple-element.323, f32[4,512,512]{1,2,0:T(8,128)} %get-tuple-element.280, f32[4,512]{1,0:T(4,128)S(1)} %get-tuple-element.281), kind=kOutput, calls=%fused_computation.48.clone.1 | convolution fusion | flops 141691392 | bytes 17318912 | tf_op jit(solution)/shard_map/while/body/eval_jaxpr/while/body/eval_jaxpr/hqk,qhd->khd/dot_general | solution.py:93
  206.9 8.4 %fusion.207 = bf16[4,512,4,64]{1,3,2,0:T(8,128)(2,1)} fusion(bf16[4,512,4,64]{1,3,2,0:T(8,128)(2,1)} %get-tuple-element.310, s32[]{:T(128)S(6)} %copy.42, f32[4,512,512]{1,2,0:T(8,128)} %fusion.205, bf16[4,512,4,64]{1,3,2,0:T(8,128)(2,1)} %get-tuple-element.322, f32[4,512,512]{1,2,0:T(8,128)} %get-tuple-element.280, f32[4,512]{1,0:T(4,128)S(1)} %get-tuple-element.281), kind=kOutput, calls=%fused_computation.50.clone.1 | convolution fusion | flops 141691392 | bytes 17318912 | tf_op jit(solution)/shard_map/while/body/eval_jaxpr/while/body/eval_jaxpr/hqk,khd->qhd/dot_general | solution.py:90
  215.3 2.8 fusion.205
  218.1 4.6 %fusion.206 = (f32[4,512]{1,0:T(4,128)S(1)}, f32[4,512,512]{1,2,0:T(8,128)}) fusion(bf16[4,512,4,64]{1,3,2,0:T(8,128)(2,1)} %get-tuple-element.323, s32[]{:T(128)S(6)} %copy.42, bf16[4,512,4,64]{1,3,2,0:T(8,128)(2,1)} %get-tuple-element.322), kind=kOutput, calls=%fused_computation.120.clone.1 | convolution fusion | flops 137363968 | bytes 4727808 | tf_op jit(solution)/shard_map/while/body/eval_jaxpr/while/body/eval_jaxpr/sub | solution.py:69
  222.7 3.6 fusion.209
  226.4 8.2 %fusion.208 = bf16[4,512,4,64]{1,3,2,0:T(8,128)(2,1)} fusion(bf16[4,512,4,64]{1,3,2,0:T(8,128)(2,1)} %get-tuple-element.311, s32[]{:T(128)S(6)} %copy.42, f32[4,512,512]{1,2,0:T(8,128)} %fusion.205, bf16[4,512,4,64]{1,3,2,0:T(8,128)(2,1)} %get-tuple-element.323, f32[4,512,512]{1,2,0:T(8,128)} %get-tuple-element.280, f32[4,512]{1,0:T(4,128)S(1)} %get-tuple-element.281), kind=kOutput, calls=%fused_computation.48.clone.1 | convolution fusion | flops 141691392 | bytes 17318912 | tf_op jit(solution)/shard_map/while/body/eval_jaxpr/while/body/eval_jaxpr/hqk,qhd->khd/dot_general | solution.py:93
  234.5 8.4 %fusion.207 = bf16[4,512,4,64]{1,3,2,0:T(8,128)(2,1)} fusion(bf16[4,512,4,64]{1,3,2,0:T(8,128)(2,1)} %get-tuple-element.310, s32[]{:T(128)S(6)} %copy.42, f32[4,512,512]{1,2,0:T(8,128)} %fusion.205, bf16[4,512,4,64]{1,3,2,0:T(8,128)(2,1)} %get-tuple-element.322, f32[4,512,512]{1,2,0:T(8,128)} %get-tuple-element.280, f32[4,512]{1,0:T(4,128)S(1)} %get-tuple-element.281), kind=kOutput, calls=%fused_computation.50.clone.1 | convolution fusion | flops 141691392 | bytes 17318912 | tf_op jit(solution)/shard_map/while/body/eval_jaxpr/while/body/eval_jaxpr/hqk,khd->qhd/dot_general | solution.py:90
  243.0 2.8 fusion.205
  245.8 4.6 %fusion.206 = (f32[4,512]{1,0:T(4,128)S(1)}, f32[4,512,512]{1,2,0:T(8,128)}) fusion(bf16[4,512,4,64]{1,3,2,0:T(8,128)(2,1)} %get-tuple-element.323, s32[]{:T(128)S(6)} %copy.42, bf16[4,512,4,64]{1,3,2,0:T(8,128)(2,1)} %get-tuple-element.322), kind=kOutput, calls=%fused_computation.120.clone.1 | convolution fusion | flops 137363968 | bytes 4727808 | tf_op jit(solution)/shard_map/while/body/eval_jaxpr/while/body/eval_jaxpr/sub | solution.py:69
  250.4 3.7 fusion.209
  254.1 8.2 %fusion.208 = bf16[4,512,4,64]{1,3,2,0:T(8,128)(2,1)} fusion(bf16[4,512,4,64]{1,3,2,0:T(8,128)(2,1)} %get-tuple-element.311, s32[]{:T(128)S(6)} %copy.42, f32[4,512,512]{1,2,0:T(8,128)} %fusion.205, bf16[4,512,4,64]{1,3,2,0:T(8,128)(2,1)} %get-tuple-element.323, f32[4,512,512]{1,2,0:T(8,128)} %get-tuple-element.280, f32[4,512]{1,0:T(4,128)S(1)} %get-tuple-element.281), kind=kOutput, calls=%fused_computation.48.clone.1 | convolution fusion | flops 141691392 | bytes 17318912 | tf_op jit(solution)/shard_map/while/body/eval_jaxpr/while/body/eval_jaxpr/hqk,qhd->khd/dot_general | solution.py:93
  262.2 8.4 %fusion.207 = bf16[4,512,4,64]{1,3,2,0:T(8,128)(2,1)} fusion(bf16[4,512,4,64]{1,3,2,0:T(8,128)(2,1)} %get-tuple-element.310, s32[]{:T(128)S(6)} %copy.42, f32[4,512,512]{1,2,0:T(8,128)} %fusion.205, bf16[4,512,4,64]{1,3,2,0:T(8,128)(2,1)} %get-tuple-element.322, f32[4,512,512]{1,2,0:T(8,128)} %get-tuple-element.280, f32[4,512]{1,0:T(4,128)S(1)} %get-tuple-element.281), kind=kOutput, calls=%fused_computation.50.clone.1 | convolution fusion | flops 141691392 | bytes 17318912 | tf_op jit(solution)/shard_map/while/body/eval_jaxpr/while/body/eval_jaxpr/hqk,khd->qhd/dot_general | solution.py:90
  270.7 7.4 %multiply_reduce_fusion.5 = (f32[512]{0:T(512)S(1)}, f32[512]{0:T(512)S(1)}, f32[512,1024]{1,0:T(8,128)S(1)}) fusion(f32[1024]{0:T(1024)S(1)} %copy-done.5, f32[512]{0:T(512)S(1)} %rsqrt.12, f32[512]{0:T(512)S(1)} %div.31, bf16[1,8,8,8,1024]{4,3,2,1,0:T(8,128)(2,1)S(1)} %get-tuple-element.183, bf16[1024,3072]{1,0:T(8,128)(2,1)} %all-gather.3.cloned.1.call-done, ...), kind=kOutput, calls=%fused_computation.104 | convolution fusion | flops 3234331648 | bytes 12595200 | tf_op jit(solution)/shard_map/dot_general | solution.py:117
  281.3 1.9 collective-permute-start.1
  283.2 67.7 %collective-permute-done.3 = bf16[1,8,8,8,1024]{4,3,2,1,0:T(8,128)(2,1)S(1)} collective-permute-done((bf16[1,8,8,8,1024]{4,3,2,1,0:T(8,128)(2,1)S(1)}, bf16[1,8,8,8,1024]{4,3,2,1,0:T(8,128)(2,1)S(1)}, u32[]{:S(2)}, u32[]{:S(2)}) %collective-permute-start.3) | collective-permute-done | bytes 1048608 | tf_op jit(solution)/shard_map/ppermute | solution.py:17
  350.8 1.3 fusion.137
  352.2 19.5 %collective-permute-done.1 = bf16[1,8,8,8,1024]{4,3,2,1,0:T(8,128)(2,1)S(1)} collective-permute-done((bf16[1,8,8,8,1024]{4,3,2,1,0:T(8,128)(2,1)S(1)}, bf16[1,8,8,8,1024]{4,3,2,1,0:T(8,128)(2,1)S(1)}, u32[]{:S(2)}, u32[]{:S(2)}) %collective-permute-start.1) | collective-permute-done | bytes 1048608 | tf_op jit(solution)/shard_map/ppermute | solution.py:17
  371.7 1.3 fusion.140
  (33 shorter events, 11.0 us)
Async XLA Ops:
  7.2 1.5 copy-start.2
  7.2 5.6 %copy-start.3 = (bf16[1,1,8,8,8,1024]{5,4,3,2,1,0:T(8,128)(2,1)S(1)}, bf16[1,1,8,8,8,1024]{5,4,3,2,1,0:T(8,128)(2,1)}, u32[]{:S(2)}) copy-start(bf16[1,1,8,8,8,1024]{5,4,3,2,1,0:T(8,128)(2,1)} %param.11) | copy-start | bytes 3145732
  7.2 98.0 %all-gather.5.cloned.1.call-start = ((), (), s32[]{:S(2)}) async-start(), calls=%async_computation.1 | async-start | bytes 3145728 | tf_op jit(solution)/shard_map/all_gather | solution.py:172
  7.9 102.6 %all-gather.3.cloned.1.call-start = ((), (), s32[]{:S(2)}) async-start(), calls=%async_computation | async-start | bytes 9437184 | tf_op jit(solution)/shard_map/all_gather | solution.py:158
  8.7 96.1 %copy-start.5 = (f32[1024]{0:T(1024)S(1)}, f32[1024]{0:T(1024)}, u32[]{:S(2)}) copy-start(f32[1024]{0:T(1024)} %param.15) | copy-start | bytes 12292
  8.7 73.0 %collective-permute-start = (bf16[1,8,8,8,1024]{4,3,2,1,0:T(8,128)(2,1)S(1)}, bf16[1,8,8,8,1024]{4,3,2,1,0:T(8,128)(2,1)S(1)}, u32[]{:S(2)}, u32[]{:S(2)}) collective-permute-start(bf16[1,8,8,8,1024]{4,3,2,1,0:T(8,128)(2,1)S(1)} %bitcast.174), channel_id=1, source_target_pairs={{0,8},{2,10},{4,12},{6,14},{8,0},{10,2},{12,4},{14,6},{1,9},{3,11}... | collective-permute-start | bytes 3145736 | tf_op jit(solution)/shard_map/ppermute | solution.py:17
  12.8 90.7 %collective-permute-start.2 = (bf16[1,8,8,8,1024]{4,3,2,1,0:T(8,128)(2,1)S(1)}, bf16[1,8,8,8,1024]{4,3,2,1,0:T(8,128)(2,1)}, u32[]{:S(2)}, u32[]{:S(2)}) collective-permute-start(bf16[1,8,8,8,1024]{4,3,2,1,0:T(8,128)(2,1)S(1)} %bitcast.176), channel_id=1, source_target_pairs={{0,8},{2,10},{4,12},{6,14},{8,0},{10,2},{12,4},{14,6},{1,9},{3,11}... | collective-permute-start | bytes 3145736 | tf_op jit(solution)/shard_map/ppermute | solution.py:17
  81.7 1.0 copy-start.4
  278.1 1.2 copy-start
  278.1 1.9 copy-start.1
  278.8 72.0 %collective-permute-start.3 = (bf16[1,8,8,8,1024]{4,3,2,1,0:T(8,128)(2,1)S(1)}, bf16[1,8,8,8,1024]{4,3,2,1,0:T(8,128)(2,1)S(1)}, u32[]{:S(2)}, u32[]{:S(2)}) collective-permute-start(bf16[1,8,8,8,1024]{4,3,2,1,0:T(8,128)(2,1)S(1)} %bitcast.169), channel_id=1, source_target_pairs={{0,8},{2,10},{4,12},{6,14},{8,0},{10,2},{12,4},{14,6},{1,9},{3,11}... | collective-permute-start | bytes 3145736 | tf_op jit(solution)/shard_map/ppermute | solution.py:17
  281.3 90.3 %collective-permute-start.1 = (bf16[1,8,8,8,1024]{4,3,2,1,0:T(8,128)(2,1)S(1)}, bf16[1,8,8,8,1024]{4,3,2,1,0:T(8,128)(2,1)S(1)}, u32[]{:S(2)}, u32[]{:S(2)}) collective-permute-start(bf16[1,8,8,8,1024]{4,3,2,1,0:T(8,128)(2,1)S(1)} %bitcast.171), channel_id=1, source_target_pairs={{0,8},{2,10},{4,12},{6,14},{8,0},{10,2},{12,4},{14,6},{1,9},{3,11}... | collective-permute-start | bytes 3145736 | tf_op jit(solution)/shard_map/ppermute | solution.py:17
Sparse Core Ops, SparseCore 0:
  9.6 13.2 all-gather.4
  24.4 17.9 all-gather.2
where the time goes:
time: 381 us; the launch traced here: 380 us
  waiting for transfers between devices  175 us (46%)
  matrix products  161 us (42%)
  local copies, waits for them, and re-layouts  15 us (4%)
  between operations  14.9 us (4%)
  other arithmetic  6.9 us (2%)
  starting transfers between devices  6.19 us (2%)
    ppermute x4, waiting for transfers between devices, passed_along(): return lax.ppermute(x, axis, [(i, (i + by) % size) for i in range(size)])  174 us
    sub x8, matrix products, probabilities(): raised = jnp.exp(scores - peak)  36.8 us
    dot_general x4, matrix products, reverse_group(): jnp.einsum('hqk,khd->qhd', grad_scores, keys, preferred_element_type=jnp....  33.7 us
    dot_general x4, matrix products, reverse_group(): jnp.einsum('hqk,qhd->khd', grad_scores, query, preferred_element_type=jnp...  32.7 us
    dot_general x4, matrix products, reverse_group(): jnp.einsum('hqk,qhd->khd', soft_low, upstream, preferred_element_type=jnp...  14.6 us
    dot_general x4, matrix products, attend_group(): jnp.einsum('hqk,khd->qhd', soft_low, values, preferred_element_type=jnp.f...  13.5 us
    dot_general x2, matrix products, contract_rows(): lax.dot_general(left, right, (((1,), (1,)), ((), ())), preferred_element_...  11.3 us
    dot_general x4, matrix products, reverse_group(): jnp.einsum('qhd,khd->hqk', upstream, values, preferred_element_type=jnp.f...  11.2 us
  transfers between devices with their start and end apart: 6, of which 4 were waited for; matrix products, arithmetic and copies ran while one was open for 3% of the time, Pallas kernels for 0%

commit v1 on v0

v1 whole, which is shorter than its diff:
```python
import jax
import jax.numpy as jnp
from jax import lax
from jax.experimental import pallas as pl
from jax.experimental.pallas import tpu as pltpu
from jax.sharding import PartitionSpec as P

YTILES = 4
HEAD_DIM = 64
EPS = 1e-05
PAIR = 2 * HEAD_DIM
SCALE = HEAD_DIM ** (-0.5)


def passed_along(x, by):
    size = lax.axis_size("space")
    return lax.ppermute(x, "space", [(i, (i + by) % size) for i in range(size)])


def nt(a, b):
    return lax.dot_general(a, b, (((1,), (1,)), ((), ())), preferred_element_type=jnp.float32)


def nn(a, b):
    return lax.dot_general(a, b, (((1,), (0,)), ((), ())), preferred_element_type=jnp.float32)


def only_head(x, head):
    lane = lax.broadcasted_iota(jnp.int32, x.shape, 1)
    keep = lane < HEAD_DIM if head == 0 else lane >= HEAD_DIM
    return jnp.where(keep, x, jnp.zeros_like(x))


def by_head(first, second):
    lane = lax.broadcasted_iota(jnp.int32, first.shape, 1)
    return jnp.where(lane < HEAD_DIM, first, second)


def attend_kernel(q_ref, k_ref, v_ref, o_ref, stats_ref):
    q, k = q_ref[...], k_ref[...]
    v_t = v_ref[...].T
    outs = []
    for head in range(2):
        scores = nt(k, only_head(q, head)) * SCALE
        peak = jnp.max(scores, axis=0, keepdims=True)
        raised = jnp.exp(scores - peak)
        inv = 1.0 / jnp.sum(raised, axis=0, keepdims=True)
        stats_ref[0, 2 * head : 2 * head + 1, :] = peak
        stats_ref[0, 2 * head + 1 : 2 * head + 2, :] = inv
        probs = (raised * inv).astype(jnp.bfloat16)
        outs.append(nn(v_t[HEAD_DIM * head : HEAD_DIM * (head + 1)], probs))
    o_ref[...] = jnp.concatenate(outs, axis=0).T.astype(jnp.bfloat16)


def reverse_kernel(q_ref, k_ref, v_ref, up_ref, stats_ref, dq_ref, dk_ref, dv_ref):
    q, k, v, up = q_ref[...], k_ref[...], v_ref[...], up_ref[...]
    k_t = k.T
    dqs, dks, dvs = [], [], []
    for head in range(2):
        scores = nt(k, only_head(q, head)) * SCALE
        peak = stats_ref[0, 2 * head : 2 * head + 1, :]
        inv = stats_ref[0, 2 * head + 1 : 2 * head + 2, :]
        probs = jnp.exp(scores - peak) * inv
        grad_probs = nt(v, only_head(up, head))
        delta = jnp.sum(grad_probs * probs, axis=0, keepdims=True)
        grad_scores = (probs * (grad_probs - delta) * SCALE).astype(jnp.bfloat16)
        dqs.append(nn(k_t[HEAD_DIM * head : HEAD_DIM * (head + 1)], grad_scores))
        dks.append(nn(grad_scores, q))
        dvs.append(nn(probs.astype(jnp.bfloat16), up))
    dq_ref[...] = jnp.concatenate(dqs, axis=0).T.astype(jnp.bfloat16)
    dk_ref[...] = by_head(*dks).astype(jnp.bfloat16)
    dv_ref[...] = by_head(*dvs).astype(jnp.bfloat16)


def attend(qkv):
    tokens, width = qkv.shape
    channels = width // 3
    pairs = channels // PAIR

    def cols(which):
        return pl.BlockSpec((tokens, PAIR), lambda i: (0, which * pairs + i))

    return pl.pallas_call(
        attend_kernel,
        grid=(pairs,),
        in_specs=[cols(0), cols(1), cols(2)],
        out_specs=[cols(0), pl.BlockSpec((1, 4, tokens), lambda i: (i, 0, 0))],
        out_shape=[
            jax.ShapeDtypeStruct((tokens, channels), jnp.bfloat16),
            jax.ShapeDtypeStruct((pairs, 4, tokens), jnp.float32),
        ],
        compiler_params=pltpu.CompilerParams(vmem_limit_bytes=40 << 20),
        cost_estimate=pl.CostEstimate(
            flops=8 * tokens * tokens * channels,
            transcendentals=tokens * tokens * channels // HEAD_DIM,
            bytes_accessed=8 * tokens * channels,
        ),
        name="attend",
    )(qkv, qkv, qkv)


def reverse(qkv, up, stats):
    tokens, width = qkv.shape
    channels = width // 3
    pairs = channels // PAIR

    def cols(which):
        return pl.BlockSpec((tokens, PAIR), lambda i: (0, which * pairs + i))

    return pl.pallas_call(
        reverse_kernel,
        grid=(pairs,),
        in_specs=[cols(0), cols(1), cols(2), cols(0), pl.BlockSpec((1, 4, tokens), lambda i: (i, 0, 0))],
        out_specs=[cols(0), cols(0), cols(0)],
        out_shape=[jax.ShapeDtypeStruct((tokens, channels), jnp.bfloat16)] * 3,
        compiler_params=pltpu.CompilerParams(vmem_limit_bytes=40 << 20),
        cost_estimate=pl.CostEstimate(
            flops=20 * tokens * tokens * channels,
            transcendentals=tokens * tokens * channels // HEAD_DIM,
            bytes_accessed=14 * tokens * channels,
        ),
        name="reverse",
    )(qkv, qkv, qkv, up, stats)


def normalise(x):
    values32 = x.astype(jnp.float32)
    center = values32 - jnp.mean(values32, axis=-1, keepdims=True)
    inverse = lax.rsqrt(jnp.mean(center * center, axis=-1, keepdims=True) + EPS)
    return center * inverse, inverse


def shards(inputs, cotangent, offsets, w_qkv, w_out, gain):
    tiled_shape = inputs.shape
    slab, channels = tiled_shape[2], tiled_shape[-1]
    inputs = inputs.reshape(-1, channels)
    cotangent = cotangent.reshape(-1, channels)
    tokens = inputs.shape[0]
    half, plane = tokens // 2, tokens // slab
    start = offsets[0]
    upper = start > slab // 2
    two = lax.axis_size("space") == 2 * YTILES
    plane_of = lax.broadcasted_iota(jnp.int32, (half, 1), 0) // plane
    foreign = jnp.where(upper, plane_of + slab // 2 >= start, plane_of < start)

    def edge(x):
        return lax.dynamic_slice_in_dim(x, jnp.where(upper, half, 0), half, 0)

    def core(x):
        return lax.dynamic_slice_in_dim(x, jnp.where(upper, 0, half), half, 0)

    def fetch(x):
        if two:
            return passed_along(edge(x), YTILES)
        return jnp.where(upper, passed_along(x[half:], YTILES), passed_along(x[:half], -YTILES))

    def give_back(x):
        if two:
            return passed_along(x, YTILES)
        return jnp.where(upper, passed_along(x, -YTILES), passed_along(x, YTILES))

    def place(edge_mine, edge_back, core_mine):
        edge_out = jnp.where(foreign, edge_back, edge_mine)
        low = jnp.where(upper, core_mine, edge_out)
        high = jnp.where(upper, edge_out, core_mine)
        return jnp.concatenate([low, high], axis=0).reshape(tiled_shape)

    in_far = fetch(inputs)
    cot_far = fetch(cotangent)
    all_qkv = lax.all_gather(w_qkv, "batch", axis=0, tiled=True)
    all_out = lax.all_gather(w_out, "batch", axis=0, tiled=True)

    def project(x):
        normed, inverse = normalise(x)
        scaled = (normed * gain).astype(jnp.bfloat16)
        return nn(scaled, all_qkv).astype(jnp.bfloat16)

    in_core, cot_core = core(inputs), core(cotangent)
    qkv_core = project(in_core)
    up_core = nt(cot_core, all_out).astype(jnp.bfloat16)
    in_edge = jnp.where(foreign, in_far, edge(inputs))
    qkv_edge = project(in_edge)
    qkv = jnp.concatenate([qkv_edge, qkv_core], axis=0)
    attended, stats = attend(qkv)
    up_edge_rows = nn(attended[:half], all_out).astype(jnp.bfloat16)
    update_back = give_back(up_edge_rows)
    update_core = nn(attended[half:], all_out).astype(jnp.bfloat16)

    cot_edge = jnp.where(foreign, cot_far, edge(cotangent))
    up = jnp.concatenate([nt(cot_edge, all_out).astype(jnp.bfloat16), up_core], axis=0)
    grads = reverse(qkv, up, stats)

    def backward(rows, x):
        total = 0.0
        for index, piece in enumerate(grads):
            total = total + nt(piece[rows], all_qkv[:, index * channels : (index + 1) * channels])
        grad_normed = total * gain
        normed, inverse = normalise(x)
        mean_grad = jnp.mean(grad_normed, axis=-1, keepdims=True)
        mean_mixed = jnp.mean(grad_normed * normed, axis=-1, keepdims=True)
        return (inverse * (grad_normed - mean_grad - normed * mean_mixed)).astype(jnp.bfloat16)

    grad_edge = backward(slice(0, half), in_edge)
    grad_back = give_back(grad_edge)
    grad_core = backward(slice(half, tokens), in_core)
    update = place(up_edge_rows, update_back, update_core)
    grad = place(grad_edge, grad_back, grad_core)
    return update, grad


def solution(mesh):
    tiles = P(("groups", "batch"), "space", None, None, None, None)
    in_specs = (tiles, tiles, P(("groups", "batch")), P("batch", None), P("batch", None), P())
    return jax.shard_map(shards, mesh=mesh, in_specs=in_specs, out_specs=(tiles, tiles), check_vma=False)
```

time: 381 us -> 139 us (0.36)
  matrix products: 161 us -> 17.7 us
  waiting for transfers between devices: 175 us -> 62.7 us
  Pallas kernels: 0 us -> 31 us
  local copies, waits for them, and re-layouts: 15 us -> 0.91 us
    ppermute x4, waiting for transfers between devices: 174 us -> 61.3 us  [passed_along(): return lax.ppermute(x, 'space', [(i, (i + by) % size) for i in range(size)])]
    dot_general x24 -> x12, matrix products: 125 us -> 17.7 us  [the longest x8 9.49 us: nt(): lax.dot_general(a, b, (((1,), (1,)), ((), ())), preferred_element_type=jn...]
    sub x8 -> x0, matrix products: 36.8 us -> none  [probabilities(): raised = jnp.exp(scores - peak)]
    pallas_call x0 -> x2, Pallas kernels: none -> 31 us  [the longest x1 18.5 us: reverse(): pl.pallas_call(reverse_kernel, grid=(pairs,), in_specs=[cols(0), cols(1),...]
    slice x4 -> x0, local copies, waits for them, and re-layouts: 6.87 us -> none  [the longest x2 4.05 us: shards(): projected[:, channels:2 * channels].astype(jnp.bfloat16)]
    another operation x4 -> x0, local copies, waits for them, and re-layouts: 4.32 us -> none
  transfers between devices with their start and end apart: 6 -> 6, of which waited for: 4 -> 3; matrix products, arithmetic and copies ran while one was open for 3% -> 9% of each run, Pallas kernels for 0% -> 13%
where the time goes in v1:
time: 139 us
  waiting for transfers between devices  62.7 us (45%)
  Pallas kernels  31 us (22%)
  matrix products  17.7 us (13%)
  between operations  15 us (11%)
  starting transfers between devices  7.26 us (5%)
  other arithmetic  4.51 us (3%)
    ppermute x4, waiting for transfers between devices, passed_along(): return lax.ppermute(x, 'space', [(i, (i + by) % size) for i in range(size)])  61.3 us
    pallas_call x1, Pallas kernels, reverse(): pl.pallas_call(reverse_kernel, grid=(pairs,), in_specs=[cols(0), cols(1),...  18.5 us
    pallas_call x1, Pallas kernels, attend(): pl.pallas_call(attend_kernel, grid=(pairs,), in_specs=[cols(0), cols(1),...  12.5 us
    dot_general x8, matrix products, nt(): lax.dot_general(a, b, (((1,), (1,)), ((), ())), preferred_element_type=jn...  9.49 us
    dot_general x4, matrix products, nn(): lax.dot_general(a, b, (((1,), (0,)), ((), ())), preferred_element_type=jn...  8.19 us
    ppermute x4, starting transfers between devices, passed_along(): return lax.ppermute(x, 'space', [(i, (i + by) % size) for i in range(size)])  7.18 us
  transfers between devices with their start and end apart: 6, of which 3 were waited for; matrix products, arithmetic and copies ran while one was open for 9% of the time, Pallas kernels for 13%

profile of v1, /device:TPU:0, one launch (start us, length us, event | category | flops | bytes accessed | tf_op | source)
XLA Modules:
  0.0 139.1 jit_solution(1554412521302261474)
XLA Ops:
  7.2 0.0 copy-start
  7.2 0.0 copy-start.1
  7.2 0.0 all-gather.5.cloned.1.call-start
  7.2 0.7 all-gather.5.cloned.1.call-update
  7.9 0.0 all-gather.3.cloned.1.call-start
  8.0 0.7 all-gather.3.cloned.1.call-update
  9.3 0.0 copy-done.1
  9.4 4.1 %collective-permute-start = (bf16[256,1024]{1,0:T(8,128)(2,1)S(1)}, bf16[256,1024]{1,0:T(8,128)(2,1)S(1)}, u32[]{:S(2)}, u32[]{:S(2)}) collective-permute-start(bf16[256,1024]{1,0:T(8,128)(2,1)S(1)} %constant_dynamic-slice_fusion.1), channel_id=1, source_target_pairs={{0,8},{2,10},{4,12},{6,14},{8,0},{10,2},{12,4},{14,6},{1,9},{3,11}... | collective-permute-start | bytes 1572872 | tf_op jit(solution)/shard_map/ppermute | solution.py:17
  13.5 0.8 constant_dynamic-slice_fusion
  14.3 0.0 collective-permute-start.2
  14.3 0.1 convert_reduce_fusion
  14.5 0.3 fusion.45
  14.8 33.9 %collective-permute-done = bf16[256,1024]{1,0:T(8,128)(2,1)S(1)} collective-permute-done((bf16[256,1024]{1,0:T(8,128)(2,1)S(1)}, bf16[256,1024]{1,0:T(8,128)(2,1)S(1)}, u32[]{:S(2)}, u32[]{:S(2)}) %collective-permute-start) | collective-permute-done | bytes 524320 | tf_op jit(solution)/shard_map/ppermute | solution.py:17
  48.7 0.3 convert_reduce_fusion.1
  49.0 0.0 copy-start.2
  49.0 0.3 fusion.51
  49.3 0.0 all-gather.5.cloned.1.call-done
  49.4 2.5 %convolution_convert_fusion.2 = bf16[256,1024]{1,0:T(8,128)(2,1)S(1)} fusion(bf16[1024,1024]{1,0:T(8,128)(2,1)} %all-gather.5.cloned.1.call-done, bf16[512,1024]{1,0:T(8,128)(2,1)S(1)} %bitcast.14, s32[]{:T(128)S(6)} %select_n.81), kind=kOutput, calls=%fused_computation.25 | convolution fusion | flops 537133056 | bytes 3145732 | tf_op jit(solution)/shard_map/dot_general | solution.py:21
  51.9 0.0 copy-start.7
  51.9 7.4 %collective-permute-done.2 = bf16[256,1024]{1,0:T(8,128)(2,1)} collective-permute-done((bf16[256,1024]{1,0:T(8,128)(2,1)}, bf16[256,1024]{1,0:T(8,128)(2,1)}, u32[]{:S(2)}, u32[]{:S(2)}) %collective-permute-start.2) | collective-permute-done | bytes 524320 | tf_op jit(solution)/shard_map/ppermute | solution.py:17
  59.2 0.0 copy-done.5
  59.2 2.0 %convolution_convert_fusion.3 = bf16[256,1024]{1,0:T(8,128)(2,1)S(1)} fusion(bf16[1024,1024]{1,0:T(8,128)(2,1)S(1)} %copy-done.5, bf16[256,1024]{1,0:T(8,128)(2,1)} %collective-permute-done.2, bf16[256,1024]{1,0:T(8,128)(2,1)} %constant_dynamic-slice_fusion, pred[256]{0:T(512)(128)(4,1)S(1)} %compare_select_fusion), kind=kOutput, calls=%fused_computation.26 | convolution fusion | flops 537395200 | bytes 3670272 | tf_op jit(solution)/shard_map/dot_general | solution.py:21
  61.2 0.1 pad_maximum_fusion.2.up_ref
  61.3 0.0 all-gather.3.cloned.1.call-done
  61.3 0.0 copy-start.3
  61.3 0.0 copy-start.4
  61.3 4.8 %convolution_convert_fusion = bf16[256,3072]{1,0:T(8,128)(2,1)S(1)} fusion(bf16[1024,3072]{1,0:T(8,128)(2,1)} %all-gather.3.cloned.1.call-done, f32[256]{0:T(256)S(1)} %add_rsqrt_fusion, f32[256]{0:T(256)S(1)} %broadcast_multiply_fusion.4, f32[1024]{0:T(1024)S(1)} %copy-done.7, bf16[512,1024]{1,0:T(8,128)(2,1)S(1)} %bitcast.19, s32[]{:T(128)S(6)} %select_n.81), kind=kOutput, calls=%fused_computation | convolution fusion | flops 1612709888 | bytes 8394756 | tf_op jit(solution)/shard_map/dot_general | solution.py:25
  66.2 1.9 %convolution_convert_fusion.1 = bf16[256,3072]{1,0:T(8,128)(2,1)S(1)} fusion(bf16[1024,3072]{1,0:T(8,128)(2,1)S(1)} %copy-done.4, bf16[256,1024]{1,0:T(8,128)(2,1)S(1)} %copy-done.3, f32[1024]{0:T(1024)S(1)} %copy-done.7, f32[256]{0:T(256)S(1)} %add_rsqrt_fusion.1, f32[256]{0:T(256)S(1)} %broadcast_multiply_fusion.5), kind=kOutput, calls=%fused_computation.1 | convolution fusion | flops 1612709888 | bytes 8394752 | tf_op jit(solution)/shard_map/dot_general | solution.py:25
  68.1 0.2 pad_maximum_fusion.q_ref.k_ref.v_ref
  68.4 12.5 %attend.1 = (bf16[512,1024]{1,0:T(8,128)(2,1)S(1)}, f32[8,4,512]{2,1,0:T(4,128)S(1)}) custom-call(bf16[512,3072]{1,0:T(8,128)(2,1)S(1)} %pad_maximum_fusion.q_ref.k_ref.v_ref, bf16[512,3072]{1,0:T(8,128)(2,1)S(1)} %pad_maximum_fusion.q_ref.k_ref.v_ref, bf16[512,3072]{1,0:T(8,128)(2,1)S(1)} %pad_maximum_fusion.q_ref.k_ref.v_ref), custom_call_target="tpu_custom_call" | custom-call | flops 2147483648 | bytes 4194304 | tf_op jit(solution)/shard_map/attend/pallas_call | solution.py:83
  80.9 0.7 convolution_convert_fusion.4
  81.6 0.1 collective-permute-start.1
  81.7 18.5 %reverse.1 = (bf16[512,1024]{1,0:T(8,128)(2,1)S(1)}, bf16[512,1024]{1,0:T(8,128)(2,1)S(1)}, bf16[512,1024]{1,0:T(8,128)(2,1)S(1)}) custom-call(bf16[512,3072]{1,0:T(8,128)(2,1)S(1)} %pad_maximum_fusion.q_ref.k_ref.v_ref, bf16[512,3072]{1,0:T(8,128)(2,1)S(1)} %pad_maximum_fusion.q_ref.k_ref.v_ref, bf16[512,3072]{1,0:T(8,128)(2,1)S(1)} %pad_maximum_fusion.q_ref.k_ref.v_ref, ...), custom_call_target="tpu_custom_call" | custom-call | flops 5368709120 | bytes 7340032 | tf_op jit(solution)/shard_map/reverse/pallas_call | solution.py:110
  100.2 0.7 fusion
  100.9 0.7 fusion.4
  101.7 1.0 fusion.74
  102.7 0.3 fusion.50
  103.1 3.0 %collective-permute-start.3 = (bf16[256,1024]{1,0:T(8,128)(2,1)S(1)}, bf16[256,1024]{1,0:T(8,128)(2,1)S(1)}, u32[]{:S(2)}, u32[]{:S(2)}) collective-permute-start(bf16[256,1024]{1,0:T(8,128)(2,1)S(1)} %fusion.50), channel_id=1, source_target_pairs={{0,8},{2,10},{4,12},{6,14},{8,0},{10,2},{12,4},{14,6},{1,9},{3,11}... | collective-permute-start | bytes 1572872 | tf_op jit(solution)/shard_map/ppermute | solution.py:17
  106.1 0.7 fusion.2
  106.8 0.7 fusion.6
  107.6 1.0 fusion.75
  108.6 0.7 convolution_convert_fusion.5
  109.3 20.0 %collective-permute-done.3 = bf16[256,1024]{1,0:T(8,128)(2,1)S(1)} collective-permute-done((bf16[256,1024]{1,0:T(8,128)(2,1)S(1)}, bf16[256,1024]{1,0:T(8,128)(2,1)S(1)}, u32[]{:S(2)}, u32[]{:S(2)}) %collective-permute-start.3) | collective-permute-done | bytes 524320 | tf_op jit(solution)/shard_map/ppermute | solution.py:17
  129.4 0.5 broadcast_select_fusion.4
  129.9 0.0 collective-permute-done.1
  129.9 0.3 broadcast_select_fusion.6
  130.1 1.0 pad_maximum_fusion.1
  131.2 1.0 pad_maximum_fusion.3
  (16 shorter events, 0.1 us)
Async XLA Ops:
  7.2 6.3 %copy-start = (bf16[1,1,8,8,8,1024]{5,4,3,2,1,0:T(8,128)(2,1)S(1)}, bf16[1,1,8,8,8,1024]{5,4,3,2,1,0:T(8,128)(2,1)}, u32[]{:S(2)}) copy-start(bf16[1,1,8,8,8,1024]{5,4,3,2,1,0:T(8,128)(2,1)} %param.7) | copy-start | bytes 3145732
  7.2 2.1 %copy-start.1 = (bf16[1,1,8,8,8,1024]{5,4,3,2,1,0:T(8,128)(2,1)S(1)}, bf16[1,1,8,8,8,1024]{5,4,3,2,1,0:T(8,128)(2,1)}, u32[]{:S(2)}) copy-start(bf16[1,1,8,8,8,1024]{5,4,3,2,1,0:T(8,128)(2,1)} %param.6) | copy-start | bytes 3145732
  7.2 42.2 %all-gather.5.cloned.1.call-start = ((), (), s32[]{:S(2)}) async-start(), calls=%async_computation.1 | async-start | bytes 3145728 | tf_op jit(solution)/shard_map/all_gather | solution.py:171
  7.9 53.4 %all-gather.3.cloned.1.call-start = ((), (), s32[]{:S(2)}) async-start(), calls=%async_computation | async-start | bytes 9437184 | tf_op jit(solution)/shard_map/all_gather | solution.py:170
  9.4 39.3 %collective-permute-start = (bf16[256,1024]{1,0:T(8,128)(2,1)S(1)}, bf16[256,1024]{1,0:T(8,128)(2,1)S(1)}, u32[]{:S(2)}, u32[]{:S(2)}) collective-permute-start(bf16[256,1024]{1,0:T(8,128)(2,1)S(1)} %constant_dynamic-slice_fusion.1), channel_id=1, source_target_pairs={{0,8},{2,10},{4,12},{6,14},{8,0},{10,2},{12,4},{14,6},{1,9},{3,11}... | collective-permute-start | bytes 1572872 | tf_op jit(solution)/shard_map/ppermute | solution.py:17
  14.3 44.9 %collective-permute-start.2 = (bf16[256,1024]{1,0:T(8,128)(2,1)}, bf16[256,1024]{1,0:T(8,128)(2,1)}, u32[]{:S(2)}, u32[]{:S(2)}) collective-permute-start(bf16[256,1024]{1,0:T(8,128)(2,1)} %constant_dynamic-slice_fusion), channel_id=1, source_target_pairs={{0,8},{2,10},{4,12},{6,14},{8,0},{10,2},{12,4},{14,6},{1,9},{3,11}... | collective-permute-start | bytes 1572872 | tf_op jit(solution)/shard_map/ppermute | solution.py:17
  49.0 10.2 %copy-start.2 = (bf16[256,1024]{1,0:T(8,128)(2,1)}, bf16[256,1024]{1,0:T(8,128)(2,1)S(1)}, u32[]{:S(2)}) copy-start(bf16[256,1024]{1,0:T(8,128)(2,1)S(1)} %get-tuple-element.19) | copy-start | bytes 1572868
  49.4 9.9 %copy-start.5 = (bf16[1024,1024]{1,0:T(8,128)(2,1)S(1)}, bf16[1024,1024]{1,0:T(8,128)(2,1)}, u32[]{:S(2)}) copy-start(bf16[1024,1024]{1,0:T(8,128)(2,1)} %all-gather.5.cloned.1.call-done) | copy-start | bytes 6291460
  51.9 9.5 %copy-start.7 = (f32[1024]{0:T(1024)S(1)}, f32[1024]{0:T(1024)}, u32[]{:S(2)}) copy-start(f32[1024]{0:T(1024)} %param.11) | copy-start | bytes 12292
  61.3 4.9 %copy-start.3 = (bf16[256,1024]{1,0:T(8,128)(2,1)S(1)}, bf16[256,1024]{1,0:T(8,128)(2,1)}, u32[]{:S(2)}) copy-start(bf16[256,1024]{1,0:T(8,128)(2,1)} %copy-done.2) | copy-start | bytes 1572868
  61.3 4.9 %copy-start.4 = (bf16[1024,3072]{1,0:T(8,128)(2,1)S(1)}, bf16[1024,3072]{1,0:T(8,128)(2,1)}, u32[]{:S(2)}) copy-start(bf16[1024,3072]{1,0:T(8,128)(2,1)} %all-gather.3.cloned.1.call-done) | copy-start | bytes 18874372
  68.3 12.5 %copy-start.6 = (bf16[1024,1024]{1,0:T(8,128)(2,1)S(1)}, bf16[1024,1024]{1,0:T(8,128)(2,1)}, u32[]{:S(2)}) copy-start(bf16[1024,1024]{1,0:T(8,128)(2,1)} %all-gather.5.cloned.1.call-done) | copy-start | bytes 6291460
  81.6 48.3 %collective-permute-start.1 = (bf16[256,1024]{1,0:T(8,128)(2,1)S(1)}, bf16[256,1024]{1,0:T(8,128)(2,1)S(1)}, u32[]{:S(2)}, u32[]{:S(2)}) collective-permute-start(bf16[256,1024]{1,0:T(8,128)(2,1)S(1)} %convolution_convert_fusion.4), channel_id=1, source_target_pairs={{0,8},{2,10},{4,12},{6,14},{8,0},{10,2},{12,4},{14,6},{1,9},{3,11}... | collective-permute-start | bytes 1572872 | tf_op jit(solution)/shard_map/ppermute | solution.py:17
  103.1 26.3 %collective-permute-start.3 = (bf16[256,1024]{1,0:T(8,128)(2,1)S(1)}, bf16[256,1024]{1,0:T(8,128)(2,1)S(1)}, u32[]{:S(2)}, u32[]{:S(2)}) collective-permute-start(bf16[256,1024]{1,0:T(8,128)(2,1)S(1)} %fusion.50), channel_id=1, source_target_pairs={{0,8},{2,10},{4,12},{6,14},{8,0},{10,2},{12,4},{14,6},{1,9},{3,11}... | collective-permute-start | bytes 1572872 | tf_op jit(solution)/shard_map/ppermute | solution.py:17
Sparse Core Ops, SparseCore 0:
  9.6 13.2 all-gather.4
  24.4 17.9 all-gather.2

commit v2 on v1

--- a/solution.py
+++ b/solution.py
@@ -149,6 +149,9 @@
     def core(x):
         return lax.dynamic_slice_in_dim(x, jnp.where(upper, 0, half), half, 0)
 
+    def after(x, *earlier):
+        return lax.optimization_barrier((x,) + earlier)[0]
+
     def fetch(x):
         if two:
             return passed_along(edge(x), YTILES)
@@ -166,7 +169,6 @@
         return jnp.concatenate([low, high], axis=0).reshape(tiled_shape)
 
     in_far = fetch(inputs)
-    cot_far = fetch(cotangent)
     all_qkv = lax.all_gather(w_qkv, "batch", axis=0, tiled=True)
     all_out = lax.all_gather(w_out, "batch", axis=0, tiled=True)
 
@@ -178,6 +180,8 @@
     in_core, cot_core = core(inputs), core(cotangent)
     qkv_core = project(in_core)
     up_core = nt(cot_core, all_out).astype(jnp.bfloat16)
+    in_far = after(in_far, qkv_core, up_core)
+    cot_far = fetch(after(cotangent, in_far))
     in_edge = jnp.where(foreign, in_far, edge(inputs))
     qkv_edge = project(in_edge)
     qkv = jnp.concatenate([qkv_edge, qkv_core], axis=0)
@@ -186,6 +190,7 @@
     update_back = give_back(up_edge_rows)
     update_core = nn(attended[half:], all_out).astype(jnp.bfloat16)
 
+    cot_far = after(cot_far, up_edge_rows)
     cot_edge = jnp.where(foreign, cot_far, edge(cotangent))
     up = jnp.concatenate([nt(cot_edge, all_out).astype(jnp.bfloat16), up_core], axis=0)
     grads = reverse(qkv, up, stats)

time: 139 us -> 143 us (1.029)
  waiting for transfers between devices: 62.7 us -> 68.7 us
    ppermute x4, waiting for transfers between devices: 61.3 us -> 41.4 us  [passed_along(): return lax.ppermute(x, 'space', [(i, (i + by) % size) for i in range(size)])]
    all_gather x1, waiting for transfers between devices: 0.02 us -> 17 us  [shards(): all_qkv = lax.all_gather(w_qkv, 'batch', axis=0, tiled=True)]
    all_gather x1, waiting for transfers between devices: 0.02 us -> 8.92 us  [shards(): all_out = lax.all_gather(w_out, 'batch', axis=0, tiled=True)]
  transfers between devices with their start and end apart: 6 -> 6, of which waited for: 3 -> 4; matrix products, arithmetic and copies ran while one was open for 9% -> 13% of each run, Pallas kernels for 13% -> 22%
where the time goes in v2:
time: 143 us
  waiting for transfers between devices  68.7 us (48%)
  Pallas kernels  31 us (22%)
  matrix products  16.4 us (11%)
  between operations  14.9 us (10%)
  starting transfers between devices  7.3 us (5%)
  other arithmetic  4.55 us (3%)
    ppermute x4, waiting for transfers between devices, passed_along(): return lax.ppermute(x, 'space', [(i, (i + by) % size) for i in range(size)])  41.4 us
    pallas_call x1, Pallas kernels, reverse(): pl.pallas_call(reverse_kernel, grid=(pairs,), in_specs=[cols(0), cols(1),...  18.5 us
    all_gather x1, waiting for transfers between devices, shards(): all_qkv = lax.all_gather(w_qkv, 'batch', axis=0, tiled=True)  17 us
    pallas_call x1, Pallas kernels, attend(): pl.pallas_call(attend_kernel, grid=(pairs,), in_specs=[cols(0), cols(1),...  12.5 us
    all_gather x1, waiting for transfers between devices, shards(): all_out = lax.all_gather(w_out, 'batch', axis=0, tiled=True)  8.92 us
    dot_general x8, matrix products, nt(): lax.dot_general(a, b, (((1,), (1,)), ((), ())), preferred_element_type=jn...  8.3 us
    dot_general x4, matrix products, nn(): lax.dot_general(a, b, (((1,), (0,)), ((), ())), preferred_element_type=jn...  8.15 us
    ppermute x4, starting transfers between devices, passed_along(): return lax.ppermute(x, 'space', [(i, (i + by) % size) for i in range(size)])  7.22 us
  transfers between devices with their start and end apart: 6, of which 4 were waited for; matrix products, arithmetic and copies ran while one was open for 13% of the time, Pallas kernels for 22%

profile of v2, /device:TPU:0, one launch (start us, length us, event | category | flops | bytes accessed | tf_op | source)
XLA Modules:
  0.0 143.0 jit_solution(928530188535809697)
XLA Ops:
  7.2 0.0 copy-start
  7.2 0.0 all-gather.5.cloned.1.call-start
  7.2 0.7 all-gather.5.cloned.1.call-update
  7.9 0.0 all-gather.3.cloned.1.call-start
  8.0 0.7 all-gather.3.cloned.1.call-update
  9.3 0.0 copy-done
  9.4 4.1 %collective-permute-start = (bf16[256,1024]{1,0:T(8,128)(2,1)S(1)}, bf16[256,1024]{1,0:T(8,128)(2,1)S(1)}, u32[]{:S(2)}, u32[]{:S(2)}) collective-permute-start(bf16[256,1024]{1,0:T(8,128)(2,1)S(1)} %constant_dynamic-slice_fusion.1), channel_id=1, source_target_pairs={{0,8},{2,10},{4,12},{6,14},{8,0},{10,2},{12,4},{14,6},{1,9},{3,11}... | collective-permute-start | bytes 1572872 | tf_op jit(solution)/shard_map/ppermute | solution.py:17
  13.5 0.1 convert_reduce_fusion.1
  13.6 0.0 copy-start.4
  13.6 0.3 fusion.51
  13.9 8.9 %all-gather.5.cloned.1.call-done = bf16[1024,1024]{1,0:T(8,128)(2,1)} async-done(((bf16[512,1024]{1,0:T(8,128)(2,1)}), bf16[1024,1024]{1,0:T(8,128)(2,1)}) %all-gather.5.cloned.1.call-update) | async-done | bytes 2097168 | tf_op jit(solution)/shard_map/all_gather | solution.py:173
  22.9 2.5 %convolution_convert_fusion.5 = bf16[256,1024]{1,0:T(8,128)(2,1)S(1)} fusion(bf16[1024,1024]{1,0:T(8,128)(2,1)} %all-gather.5.cloned.1.call-done, bf16[512,1024]{1,0:T(8,128)(2,1)} %bitcast.22, s32[]{:T(128)S(6)} %select_n.80), kind=kOutput, calls=%fused_computation.28 | convolution fusion | flops 537133056 | bytes 3145732 | tf_op jit(solution)/shard_map/dot_general | solution.py:21
  25.4 17.0 %all-gather.3.cloned.1.call-done = bf16[1024,3072]{1,0:T(8,128)(2,1)} async-done(((bf16[512,3072]{1,0:T(8,128)(2,1)}), bf16[1024,3072]{1,0:T(8,128)(2,1)}) %all-gather.3.cloned.1.call-update) | async-done | bytes 6291472 | tf_op jit(solution)/shard_map/all_gather | solution.py:172
  42.4 0.0 copy-done.4
  42.4 0.0 copy-start.1
  42.4 4.8 %convolution_convert_fusion.1 = bf16[256,3072]{1,0:T(8,128)(2,1)S(1)} fusion(bf16[1024,3072]{1,0:T(8,128)(2,1)} %all-gather.3.cloned.1.call-done, f32[1024]{0:T(1024)S(1)} %copy-done.4, f32[256]{0:T(256)S(1)} %add_rsqrt_fusion.1, f32[256]{0:T(256)S(1)} %broadcast_multiply_fusion.5, bf16[512,1024]{1,0:T(8,128)(2,1)S(1)} %bitcast.16, s32[]{:T(128)S(6)} %select_n.80), kind=kOutput, calls=%fused_computation.1 | convolution fusion | flops 1612709888 | bytes 8394756 | tf_op jit(solution)/shard_map/dot_general | solution.py:25
  47.2 0.0 collective-permute-done
  47.2 0.0 copy-done.1
  47.3 0.3 convert_reduce_fusion
  47.6 0.3 fusion.45
  47.9 2.7 %collective-permute-start.2 = (bf16[256,1024]{1,0:T(8,128)(2,1)S(1)}, bf16[256,1024]{1,0:T(8,128)(2,1)S(1)}, u32[]{:S(2)}, u32[]{:S(2)}) collective-permute-start(bf16[256,1024]{1,0:T(8,128)(2,1)S(1)} %constant_dynamic-slice_fusion), channel_id=1, source_target_pairs={{0,8},{2,10},{4,12},{6,14},{8,0},{10,2},{12,4},{14,6},{1,9},{3,11}... | collective-permute-start | bytes 1572872 | tf_op jit(solution)/shard_map/ppermute | solution.py:17
  50.6 0.0 copy-done.2
  50.6 1.9 %convolution_convert_fusion = bf16[256,3072]{1,0:T(8,128)(2,1)S(1)} fusion(bf16[1024,3072]{1,0:T(8,128)(2,1)S(1)} %copy-done.2, bf16[256,1024]{1,0:T(8,128)(2,1)S(1)} %get-tuple-element.25, f32[256]{0:T(256)S(1)} %add_rsqrt_fusion, f32[256]{0:T(256)S(1)} %broadcast_multiply_fusion.4, f32[1024]{0:T(1024)S(1)} %copy-done.4), kind=kOutput, calls=%fused_computation | convolution fusion | flops 1612709888 | bytes 8394752 | tf_op jit(solution)/shard_map/dot_general | solution.py:25
  52.5 0.2 pad_maximum_fusion.q_ref.k_ref.v_ref
  52.7 0.0 copy-start.3
  52.7 12.5 %attend.1 = (bf16[512,1024]{1,0:T(8,128)(2,1)S(1)}, f32[8,4,512]{2,1,0:T(4,128)S(1)}) custom-call(bf16[512,3072]{1,0:T(8,128)(2,1)S(1)} %pad_maximum_fusion.q_ref.k_ref.v_ref, bf16[512,3072]{1,0:T(8,128)(2,1)S(1)} %pad_maximum_fusion.q_ref.k_ref.v_ref, bf16[512,3072]{1,0:T(8,128)(2,1)S(1)} %pad_maximum_fusion.q_ref.k_ref.v_ref), custom_call_target="tpu_custom_call" | custom-call | flops 2147483648 | bytes 4194304 | tf_op jit(solution)/shard_map/attend/pallas_call | solution.py:83
  65.2 0.0 copy-done.3
  65.2 0.7 convolution_convert_fusion.3
  66.0 0.3 collective-permute-start.1
  66.3 0.7 convolution_convert_fusion.4
  67.0 19.1 %collective-permute-done.2 = bf16[256,1024]{1,0:T(8,128)(2,1)S(1)} collective-permute-done((bf16[256,1024]{1,0:T(8,128)(2,1)S(1)}, bf16[256,1024]{1,0:T(8,128)(2,1)S(1)}, u32[]{:S(2)}, u32[]{:S(2)}) %collective-permute-start.2) | collective-permute-done | bytes 524320 | tf_op jit(solution)/shard_map/ppermute | solution.py:17
  86.1 0.8 convolution_convert_fusion.2
  86.8 0.1 pad_maximum_fusion.2.up_ref
  86.9 18.5 %reverse.1 = (bf16[512,1024]{1,0:T(8,128)(2,1)S(1)}, bf16[512,1024]{1,0:T(8,128)(2,1)S(1)}, bf16[512,1024]{1,0:T(8,128)(2,1)S(1)}) custom-call(bf16[512,3072]{1,0:T(8,128)(2,1)S(1)} %pad_maximum_fusion.q_ref.k_ref.v_ref, bf16[512,3072]{1,0:T(8,128)(2,1)S(1)} %pad_maximum_fusion.q_ref.k_ref.v_ref, bf16[512,3072]{1,0:T(8,128)(2,1)S(1)} %pad_maximum_fusion.q_ref.k_ref.v_ref, ...), custom_call_target="tpu_custom_call" | custom-call | flops 5368709120 | bytes 7340032 | tf_op jit(solution)/shard_map/reverse/pallas_call | solution.py:110
  105.5 0.7 fusion.4
  106.2 0.7 fusion
  107.0 1.0 fusion.76
  108.0 0.3 fusion.44
  108.4 0.1 collective-permute-start.3
  108.5 0.7 fusion.6
  109.2 0.7 fusion.2
  109.9 1.0 fusion.77
  111.0 22.3 %collective-permute-done.3 = bf16[256,1024]{1,0:T(8,128)(2,1)S(1)} collective-permute-done((bf16[256,1024]{1,0:T(8,128)(2,1)S(1)}, bf16[256,1024]{1,0:T(8,128)(2,1)S(1)}, u32[]{:S(2)}, u32[]{:S(2)}) %collective-permute-start.3) | collective-permute-done | bytes 524320 | tf_op jit(solution)/shard_map/ppermute | solution.py:17
  133.3 0.5 broadcast_select_fusion.4
  133.8 0.0 collective-permute-done.1
  133.8 0.3 broadcast_select_fusion.6
  134.1 1.0 pad_maximum_fusion.1
  135.2 1.0 pad_maximum_fusion.3
  (10 shorter events, 0.1 us)
Async XLA Ops:
  7.2 2.1 %copy-start = (bf16[1,1,8,8,8,1024]{5,4,3,2,1,0:T(8,128)(2,1)S(1)}, bf16[1,1,8,8,8,1024]{5,4,3,2,1,0:T(8,128)(2,1)}, u32[]{:S(2)}) copy-start(bf16[1,1,8,8,8,1024]{5,4,3,2,1,0:T(8,128)(2,1)} %param.6) | copy-start | bytes 3145732
  7.2 15.7 %all-gather.5.cloned.1.call-start = ((), (), s32[]{:S(2)}) async-start(), calls=%async_computation.1 | async-start | bytes 3145728 | tf_op jit(solution)/shard_map/all_gather | solution.py:173
  7.9 34.5 %all-gather.3.cloned.1.call-start = ((), (), s32[]{:S(2)}) async-start(), calls=%async_computation | async-start | bytes 9437184 | tf_op jit(solution)/shard_map/all_gather | solution.py:172
  9.4 37.8 %collective-permute-start = (bf16[256,1024]{1,0:T(8,128)(2,1)S(1)}, bf16[256,1024]{1,0:T(8,128)(2,1)S(1)}, u32[]{:S(2)}, u32[]{:S(2)}) collective-permute-start(bf16[256,1024]{1,0:T(8,128)(2,1)S(1)} %constant_dynamic-slice_fusion.1), channel_id=1, source_target_pairs={{0,8},{2,10},{4,12},{6,14},{8,0},{10,2},{12,4},{14,6},{1,9},{3,11}... | collective-permute-start | bytes 1572872 | tf_op jit(solution)/shard_map/ppermute | solution.py:17
  13.6 28.8 %copy-start.4 = (f32[1024]{0:T(1024)S(1)}, f32[1024]{0:T(1024)}, u32[]{:S(2)}) copy-start(f32[1024]{0:T(1024)} %param.11) | copy-start | bytes 12292
  42.4 4.9 %copy-start.1 = (bf16[1,1,8,8,8,1024]{5,4,3,2,1,0:T(8,128)(2,1)S(1)}, bf16[1,1,8,8,8,1024]{5,4,3,2,1,0:T(8,128)(2,1)}, u32[]{:S(2)}) copy-start(bf16[1,1,8,8,8,1024]{5,4,3,2,1,0:T(8,128)(2,1)} %param.7) | copy-start | bytes 3145732
  42.4 8.3 %copy-start.2 = (bf16[1024,3072]{1,0:T(8,128)(2,1)S(1)}, bf16[1024,3072]{1,0:T(8,128)(2,1)}, u32[]{:S(2)}) copy-start(bf16[1024,3072]{1,0:T(8,128)(2,1)} %all-gather.3.cloned.1.call-done) | copy-start | bytes 18874372
  47.9 38.2 %collective-permute-start.2 = (bf16[256,1024]{1,0:T(8,128)(2,1)S(1)}, bf16[256,1024]{1,0:T(8,128)(2,1)S(1)}, u32[]{:S(2)}, u32[]{:S(2)}) collective-permute-start(bf16[256,1024]{1,0:T(8,128)(2,1)S(1)} %constant_dynamic-slice_fusion), channel_id=1, source_target_pairs={{0,8},{2,10},{4,12},{6,14},{8,0},{10,2},{12,4},{14,6},{1,9},{3,11}... | collective-permute-start | bytes 1572872 | tf_op jit(solution)/shard_map/ppermute | solution.py:17
  52.7 12.5 %copy-start.3 = (bf16[1024,1024]{1,0:T(8,128)(2,1)S(1)}, bf16[1024,1024]{1,0:T(8,128)(2,1)}, u32[]{:S(2)}) copy-start(bf16[1024,1024]{1,0:T(8,128)(2,1)} %all-gather.5.cloned.1.call-done) | copy-start | bytes 6291460
  66.0 67.9 %collective-permute-start.1 = (bf16[256,1024]{1,0:T(8,128)(2,1)S(1)}, bf16[256,1024]{1,0:T(8,128)(2,1)S(1)}, u32[]{:S(2)}, u32[]{:S(2)}) collective-permute-start(bf16[256,1024]{1,0:T(8,128)(2,1)S(1)} %convolution_convert_fusion.3), channel_id=1, source_target_pairs={{0,8},{2,10},{4,12},{6,14},{8,0},{10,2},{12,4},{14,6},{1,9},{3,11}... | collective-permute-start | bytes 1572872 | tf_op jit(solution)/shard_map/ppermute | solution.py:17
  108.4 24.9 %collective-permute-start.3 = (bf16[256,1024]{1,0:T(8,128)(2,1)S(1)}, bf16[256,1024]{1,0:T(8,128)(2,1)S(1)}, u32[]{:S(2)}, u32[]{:S(2)}) collective-permute-start(bf16[256,1024]{1,0:T(8,128)(2,1)S(1)} %fusion.44), channel_id=1, source_target_pairs={{0,8},{2,10},{4,12},{6,14},{8,0},{10,2},{12,4},{14,6},{1,9},{3,11}... | collective-permute-start | bytes 1572872 | tf_op jit(solution)/shard_map/ppermute | solution.py:17
Sparse Core Ops, SparseCore 0:
  9.6 13.2 all-gather.4
  24.4 17.9 all-gather.2

commit v3 on v2

--- a/solution.py
+++ b/solution.py
@@ -37,11 +37,11 @@
 
 
 def attend_kernel(q_ref, k_ref, v_ref, o_ref, stats_ref):
-    q, k = q_ref[...], k_ref[...]
+    q, k = q_ref[...] * SCALE, k_ref[...]
     v_t = v_ref[...].T
     outs = []
     for head in range(2):
-        scores = nt(k, only_head(q, head)) * SCALE
+        scores = nt(k, only_head(q, head))
         peak = jnp.max(scores, axis=0, keepdims=True)
         raised = jnp.exp(scores - peak)
         inv = 1.0 / jnp.sum(raised, axis=0, keepdims=True)
@@ -53,17 +53,17 @@
 
 
 def reverse_kernel(q_ref, k_ref, v_ref, up_ref, stats_ref, dq_ref, dk_ref, dv_ref):
-    q, k, v, up = q_ref[...], k_ref[...], v_ref[...], up_ref[...]
-    k_t = k.T
+    q, k, v, up = q_ref[...] * SCALE, k_ref[...], v_ref[...], up_ref[...]
+    k_t = (k * SCALE).T
     dqs, dks, dvs = [], [], []
     for head in range(2):
-        scores = nt(k, only_head(q, head)) * SCALE
+        scores = nt(k, only_head(q, head))
         peak = stats_ref[0, 2 * head : 2 * head + 1, :]
         inv = stats_ref[0, 2 * head + 1 : 2 * head + 2, :]
         probs = jnp.exp(scores - peak) * inv
         grad_probs = nt(v, only_head(up, head))
         delta = jnp.sum(grad_probs * probs, axis=0, keepdims=True)
-        grad_scores = (probs * (grad_probs - delta) * SCALE).astype(jnp.bfloat16)
+        grad_scores = (probs * (grad_probs - delta)).astype(jnp.bfloat16)
         dqs.append(nn(k_t[HEAD_DIM * head : HEAD_DIM * (head + 1)], grad_scores))
         dks.append(nn(grad_scores, q))
         dvs.append(nn(probs.astype(jnp.bfloat16), up))
@@ -168,9 +168,16 @@
         high = jnp.where(upper, edge_out, core_mine)
         return jnp.concatenate([low, high], axis=0).reshape(tiled_shape)
 
+    first = lax.axis_index("batch") == 0
+
+    def whole(own, other):
+        return jnp.concatenate([jnp.where(first, own, other), jnp.where(first, other, own)], axis=0)
+
+    other_qkv = lax.ppermute(w_qkv, "batch", [(0, 1), (1, 0)])
     in_far = fetch(inputs)
-    all_qkv = lax.all_gather(w_qkv, "batch", axis=0, tiled=True)
-    all_out = lax.all_gather(w_out, "batch", axis=0, tiled=True)
+    other_out = lax.ppermute(w_out, "batch", [(0, 1), (1, 0)])
+    all_qkv = whole(w_qkv, other_qkv)
+    all_out = whole(w_out, other_out)
 
     def project(x):
         normed, inverse = normalise(x)

time: 143 us -> 122 us (0.85)
  between operations: 14.9 us -> 1.52 us
  waiting for transfers between devices: 68.7 us -> 57.1 us
  other arithmetic: 4.55 us -> 9.56 us
  matrix products: 16.4 us -> 12.4 us
  local copies, waits for them, and re-layouts: 0.1 us -> 3.06 us
    all_gather x2 -> x0, waiting for transfers between devices: 25.9 us -> none  [the longest x1 17 us: shards(): all_qkv = lax.all_gather(w_qkv, 'batch', axis=0, tiled=True)]
    ppermute x4, waiting for transfers between devices: 41.4 us -> 57.1 us  [passed_along(): return lax.ppermute(x, 'space', [(i, (i + by) % size) for i in range(size)])]
    reduce_sum x2, other arithmetic: 0.45 us -> 2.63 us  [normalise(): center = values32 - jnp.mean(values32, axis=-1, keepdims=True)]
    dot_general x4, matrix products: 8.15 us -> 6 us  [nn(): lax.dot_general(a, b, (((1,), (0,)), ((), ())), preferred_element_type=jn...]
    select_n x0 -> x2, other arithmetic: none -> 2.09 us  [whole(): jnp.where(first, own, other)]
    dot_general x8, matrix products: 8.3 us -> 6.37 us  [nt(): lax.dot_general(a, b, (((1,), (1,)), ((), ())), preferred_element_type=jn...]
    dynamic_slice x2, local copies, waits for them, and re-layouts: 0.08 us -> 1.91 us  [edge(): return lax.dynamic_slice_in_dim(x, jnp.where(upper, half, 0), half, 0)]
  transfers between devices with their start and end apart: 6 -> 6, of which waited for: 4 -> 3; matrix products, arithmetic and copies ran while one was open for 13% -> 16% of each run, Pallas kernels for 22% -> 25%
where the time goes in v3:
time: 122 us
  waiting for transfers between devices  57.1 us (47%)
  Pallas kernels  30.3 us (25%)
  matrix products  12.4 us (10%)
  other arithmetic  9.56 us (8%)
  starting transfers between devices  7.7 us (6%)
  local copies, waits for them, and re-layouts  3.06 us (3%)
  between operations  1.52 us (1%)
    ppermute x4, waiting for transfers between devices, passed_along(): return lax.ppermute(x, 'space', [(i, (i + by) % size) for i in range(size)])  57.1 us
    pallas_call x1, Pallas kernels, reverse(): pl.pallas_call(reverse_kernel, grid=(pairs,), in_specs=[cols(0), cols(1),...  18.5 us
    pallas_call x1, Pallas kernels, attend(): pl.pallas_call(attend_kernel, grid=(pairs,), in_specs=[cols(0), cols(1),...  11.8 us
    ppermute x4, starting transfers between devices, passed_along(): return lax.ppermute(x, 'space', [(i, (i + by) % size) for i in range(size)])  7.11 us
    dot_general x8, matrix products, nt(): lax.dot_general(a, b, (((1,), (1,)), ((), ())), preferred_element_type=jn...  6.37 us
    dot_general x4, matrix products, nn(): lax.dot_general(a, b, (((1,), (0,)), ((), ())), preferred_element_type=jn...  6 us
    reduce_sum x2, other arithmetic, normalise(): center = values32 - jnp.mean(values32, axis=-1, keepdims=True)  2.63 us
  transfers between devices with their start and end apart: 6, of which 3 were waited for; matrix products, arithmetic and copies ran while one was open for 16% of the time, Pallas kernels for 25%

profile of v3, /device:TPU:0, one launch (start us, length us, event | category | flops | bytes accessed | tf_op | source)
XLA Modules:
  0.0 121.6 jit_solution(6414320406436242036)
XLA Ops:
  0.6 0.5 collective-permute-start.1
  1.1 0.1 collective-permute-start.2
  1.9 1.9 %constant_dynamic-slice_fusion.1 = bf16[256,1024]{1,0:T(8,128)(2,1)} fusion(bf16[512,1024]{1,0:T(8,128)(2,1)} %bitcast.7, s32[]{:T(128)S(6)} %select_n.103), kind=kLoop, calls=%fused_computation.98 | loop fusion | bytes 1048580 | tf_op jit(solution)/shard_map/dynamic_slice | solution.py:147
  3.8 4.0 %collective-permute-start = (bf16[256,1024]{1,0:T(8,128)(2,1)}, bf16[256,1024]{1,0:T(8,128)(2,1)}, u32[]{:S(2)}, u32[]{:S(2)}) collective-permute-start(bf16[256,1024]{1,0:T(8,128)(2,1)} %constant_dynamic-slice_fusion.1), channel_id=1, source_target_pairs={{0,8},{2,10},{4,12},{6,14},{8,0},{10,2},{12,4},{14,6},{1,9},{3,11}... | collective-permute-start | bytes 1572872 | tf_op jit(solution)/shard_map/ppermute | solution.py:17
  7.8 0.0 copy-start.2
  7.8 1.3 %convert_reduce_fusion.1 = f32[256]{0:T(256)S(1)} fusion(bf16[512,1024]{1,0:T(8,128)(2,1)} %bitcast.8, s32[]{:T(128)S(6)} %select_n.104), kind=kLoop, calls=%fused_computation.27 | loop fusion | flops 524032 | bytes 525316 | tf_op jit(solution)/shard_map/reduce_sum | solution.py:128
  9.1 1.3 %fusion.32 = f32[256]{0:T(256)S(1)} fusion(f32[256]{0:T(256)S(1)} %broadcast_multiply_fusion.5, bf16[512,1024]{1,0:T(8,128)(2,1)} %bitcast.9, s32[]{:T(128)S(6)} %select_n.104), kind=kLoop, calls=%fused_computation.53 | loop fusion | flops 1048320 | bytes 526340 | tf_op jit(solution)/shard_map/reduce_sum | solution.py:129
  10.4 0.0 collective-permute-done.2
  10.4 1.7 %broadcast_select_fusion.3 = (bf16[512,1024]{1,0:T(8,128)(2,1)S(1)}, bf16[512,1024]{1,0:T(8,128)(2,1)S(1)}) fusion(bf16[512,1024]{1,0:T(8,128)(2,1)} %param.10, bf16[512,1024]{1,0:T(8,128)(2,1)} %collective-permute-done.2, pred[]{:T(512)S(6)} %eq.3), kind=kLoop, calls=%fused_computation.58 | loop fusion | flops 1048576 | bytes 4194305 | tf_op jit(solution)/shard_map/jit(_where)/select_n | solution.py:174
  12.1 0.0 copy-start.1
  12.1 0.0 copy-done.2
  12.1 0.7 convolution_convert_fusion.3
  12.9 0.0 copy-start
  12.9 0.0 copy-start.3
  12.9 0.0 collective-permute-done.1
  12.9 1.1 copy-done.1
  14.0 0.4 broadcast_select_fusion.1
  14.4 0.1 copy-done
  14.5 0.0 copy-done.3
  14.5 2.2 %fusion.2 = bf16[256,3072]{1,0:T(8,128)(2,1)S(1)} fusion(bf16[512,3072]{1,0:T(8,128)(2,1)S(1)} %get-tuple-element.27, bf16[512,3072]{1,0:T(8,128)(2,1)S(1)} %get-tuple-element.26, f32[1024]{0:T(1024)S(1)} %copy-done.3, f32[256]{0:T(256)S(1)} %add_rsqrt_fusion.1, f32[256]{0:T(256)S(1)} %broadcast_multiply_fusion.5, bf16[512,1024]{1,0:T(8,128)(2,1)S(1)} %bitcast.10, ...), kind=kOutput, calls=%fused_computation.9 | convolution fusion | flops 1625292800 | bytes 8394756 | tf_op jit(solution)/shard_map/dot_general | solution.py:25
  16.7 14.8 %collective-permute-done = bf16[256,1024]{1,0:T(8,128)(2,1)} collective-permute-done((bf16[256,1024]{1,0:T(8,128)(2,1)}, bf16[256,1024]{1,0:T(8,128)(2,1)}, u32[]{:S(2)}, u32[]{:S(2)}) %collective-permute-start) | collective-permute-done | bytes 524320 | tf_op jit(solution)/shard_map/ppermute | solution.py:17
  31.5 1.4 %convert_reduce_fusion = (f32[256]{0:T(256)S(1)}, bf16[256,1024]{1,0:T(8,128)(2,1)S(1)}) fusion(bf16[256,1024]{1,0:T(8,128)(2,1)} %collective-permute-done, pred[256]{0:T(512)(128)(4,1)S(1)} %compare_select_fusion, bf16[512,1024]{1,0:T(8,128)(2,1)S(1)} %bitcast.11, s32[]{:T(128)S(6)} %select_n.103), kind=kLoop, calls=%fused_computation.25 | loop fusion | flops 786176 | bytes 1574148 | tf_op jit(solution)/shard_map/reduce_sum | solution.py:128
  32.9 0.3 fusion.26
  33.2 0.1 collective-permute-start.4
  33.3 2.2 %fusion.3 = bf16[256,3072]{1,0:T(8,128)(2,1)S(1)} fusion(bf16[512,3072]{1,0:T(8,128)(2,1)S(1)} %get-tuple-element.27, bf16[512,3072]{1,0:T(8,128)(2,1)S(1)} %get-tuple-element.26, bf16[256,1024]{1,0:T(8,128)(2,1)S(1)} %get-tuple-element.25, f32[256]{0:T(256)S(1)} %add_rsqrt_fusion, f32[256]{0:T(256)S(1)} %broadcast_multiply_fusion.4, f32[1024]{0:T(1024)S(1)} %copy-done.3), kind=kOutput, calls=%fused_computation.10 | convolution fusion | flops 1625292800 | bytes 8394752 | tf_op jit(solution)/shard_map/dot_general | solution.py:25
  35.5 0.2 pad_maximum_fusion.7.q_ref.k_ref.v_ref
  35.7 11.8 %attend.1 = (bf16[512,1024]{1,0:T(8,128)(2,1)S(1)}, f32[8,4,512]{2,1,0:T(4,128)S(1)}) custom-call(bf16[512,3072]{1,0:T(8,128)(2,1)S(1)} %pad_maximum_fusion.7.q_ref.k_ref.v_ref, bf16[512,3072]{1,0:T(8,128)(2,1)S(1)} %pad_maximum_fusion.7.q_ref.k_ref.v_ref, bf16[512,3072]{1,0:T(8,128)(2,1)S(1)} %pad_maximum_fusion.7.q_ref.k_ref.v_ref), custom_call_target="tpu_custom_call" | custom-call | flops 2147483648 | bytes 4194304 | tf_op jit(solution)/shard_map/attend/pallas_call | solution.py:83
  47.6 0.7 convolution_convert_fusion.1
  48.3 3.0 %collective-permute-start.3 = (bf16[256,1024]{1,0:T(8,128)(2,1)S(1)}, bf16[256,1024]{1,0:T(8,128)(2,1)S(1)}, u32[]{:S(2)}, u32[]{:S(2)}) collective-permute-start(bf16[256,1024]{1,0:T(8,128)(2,1)S(1)} %convolution_convert_fusion.1), channel_id=1, source_target_pairs={{0,8},{2,10},{4,12},{6,14},{8,0},{10,2},{12,4},{14,6},{1,9},{3,11}... | collective-permute-start | bytes 1572872 | tf_op jit(solution)/shard_map/ppermute | solution.py:17
  51.2 20.2 %collective-permute-done.4 = bf16[256,1024]{1,0:T(8,128)(2,1)S(1)} collective-permute-done((bf16[256,1024]{1,0:T(8,128)(2,1)S(1)}, bf16[256,1024]{1,0:T(8,128)(2,1)S(1)}, u32[]{:S(2)}, u32[]{:S(2)}) %collective-permute-start.4) | collective-permute-done | bytes 524320 | tf_op jit(solution)/shard_map/ppermute | solution.py:17
  71.5 0.7 convolution_convert_fusion
  72.2 0.1 pad_maximum_fusion.10.up_ref
  72.3 18.5 %reverse.1 = (bf16[512,1024]{1,0:T(8,128)(2,1)S(1)}, bf16[512,1024]{1,0:T(8,128)(2,1)S(1)}, bf16[512,1024]{1,0:T(8,128)(2,1)S(1)}) custom-call(bf16[512,3072]{1,0:T(8,128)(2,1)S(1)} %pad_maximum_fusion.7.q_ref.k_ref.v_ref, bf16[512,3072]{1,0:T(8,128)(2,1)S(1)} %pad_maximum_fusion.7.q_ref.k_ref.v_ref, ...), custom_call_target="tpu_custom_call" | custom-call | flops 5368709120 | bytes 7340032 | tf_op jit(solution)/shard_map/reverse/pallas_call | solution.py:110
  90.8 0.7 fusion.37
  91.5 0.7 fusion.42
  92.2 0.7 fusion.35
  93.0 0.7 fusion.40
  93.7 1.0 fusion.69
  94.7 0.3 fusion.25
  95.1 0.1 collective-permute-start.5
  95.1 1.0 fusion.70
  96.1 22.1 %collective-permute-done.5 = bf16[256,1024]{1,0:T(8,128)(2,1)S(1)} collective-permute-done((bf16[256,1024]{1,0:T(8,128)(2,1)S(1)}, bf16[256,1024]{1,0:T(8,128)(2,1)S(1)}, u32[]{:S(2)}, u32[]{:S(2)}) %collective-permute-start.5) | collective-permute-done | bytes 524320 | tf_op jit(solution)/shard_map/ppermute | solution.py:17
  118.2 0.5 broadcast_select_fusion.8
  118.7 0.0 collective-permute-done.3
  118.7 0.8 broadcast_select_fusion.10
  119.5 1.0 pad_maximum_fusion.9
  120.6 1.0 pad_maximum_fusion.11
  (8 shorter events, 0.1 us)
Async XLA Ops:
  0.6 12.3 %collective-permute-start.1 = (bf16[512,3072]{1,0:T(8,128)(2,1)}, bf16[512,3072]{1,0:T(8,128)(2,1)S(1)}, u32[]{:S(2)}, u32[]{:S(2)}) collective-permute-start(bf16[512,3072]{1,0:T(8,128)(2,1)} %param.9), channel_id=1, source_target_pairs={{0,1},{1,0},{2,3},{3,2},{4,5},{5,4},{6,7},{7,6},{8,9},{9,8},{10,11... | collective-permute-start | bytes 9437192 | tf_op jit(solution)/shard_map/ppermute | solution.py:176
  1.1 9.3 %collective-permute-start.2 = (bf16[512,1024]{1,0:T(8,128)(2,1)}, bf16[512,1024]{1,0:T(8,128)(2,1)}, u32[]{:S(2)}, u32[]{:S(2)}) collective-permute-start(bf16[512,1024]{1,0:T(8,128)(2,1)} %param.10), channel_id=1, source_target_pairs={{0,1},{1,0},{2,3},{3,2},{4,5},{5,4},{6,7},{7,6},{8,9},{9,8},{10,11... | collective-permute-start | bytes 3145736 | tf_op jit(solution)/shard_map/ppermute | solution.py:178
  3.8 27.7 %collective-permute-start = (bf16[256,1024]{1,0:T(8,128)(2,1)}, bf16[256,1024]{1,0:T(8,128)(2,1)}, u32[]{:S(2)}, u32[]{:S(2)}) collective-permute-start(bf16[256,1024]{1,0:T(8,128)(2,1)} %constant_dynamic-slice_fusion.1), channel_id=1, source_target_pairs={{0,8},{2,10},{4,12},{6,14},{8,0},{10,2},{12,4},{14,6},{1,9},{3,11}... | collective-permute-start | bytes 1572872 | tf_op jit(solution)/shard_map/ppermute | solution.py:17
  7.8 4.4 %copy-start.2 = (bf16[1,1,8,8,8,1024]{5,4,3,2,1,0:T(8,128)(2,1)S(1)}, bf16[1,1,8,8,8,1024]{5,4,3,2,1,0:T(8,128)(2,1)}, u32[]{:S(2)}) copy-start(bf16[1,1,8,8,8,1024]{5,4,3,2,1,0:T(8,128)(2,1)} %param.7) | copy-start | bytes 3145732
  12.1 1.9 %copy-start.1 = (bf16[512,3072]{1,0:T(8,128)(2,1)S(1)}, bf16[512,3072]{1,0:T(8,128)(2,1)}, u32[]{:S(2)}) copy-start(bf16[512,3072]{1,0:T(8,128)(2,1)} %param.9) | copy-start | bytes 9437188
  12.9 1.6 %copy-start = (bf16[1,1,8,8,8,1024]{5,4,3,2,1,0:T(8,128)(2,1)S(1)}, bf16[1,1,8,8,8,1024]{5,4,3,2,1,0:T(8,128)(2,1)}, u32[]{:S(2)}) copy-start(bf16[1,1,8,8,8,1024]{5,4,3,2,1,0:T(8,128)(2,1)} %param.6) | copy-start | bytes 3145732
  12.9 1.6 %copy-start.3 = (f32[1024]{0:T(1024)S(1)}, f32[1024]{0:T(1024)}, u32[]{:S(2)}) copy-start(f32[1024]{0:T(1024)} %param.11) | copy-start | bytes 12292
  33.2 38.3 %collective-permute-start.4 = (bf16[256,1024]{1,0:T(8,128)(2,1)S(1)}, bf16[256,1024]{1,0:T(8,128)(2,1)S(1)}, u32[]{:S(2)}, u32[]{:S(2)}) collective-permute-start(bf16[256,1024]{1,0:T(8,128)(2,1)S(1)} %constant_dynamic-slice_fusion), channel_id=1, source_target_pairs={{0,8},{2,10},{4,12},{6,14},{8,0},{10,2},{12,4},{14,6},{1,9},{3,11}... | collective-permute-start | bytes 1572872 | tf_op jit(solution)/shard_map/ppermute | solution.py:17
  48.3 70.4 %collective-permute-start.3 = (bf16[256,1024]{1,0:T(8,128)(2,1)S(1)}, bf16[256,1024]{1,0:T(8,128)(2,1)S(1)}, u32[]{:S(2)}, u32[]{:S(2)}) collective-permute-start(bf16[256,1024]{1,0:T(8,128)(2,1)S(1)} %convolution_convert_fusion.1), channel_id=1, source_target_pairs={{0,8},{2,10},{4,12},{6,14},{8,0},{10,2},{12,4},{14,6},{1,9},{3,11}... | collective-permute-start | bytes 1572872 | tf_op jit(solution)/shard_map/ppermute | solution.py:17
  95.1 23.2 %collective-permute-start.5 = (bf16[256,1024]{1,0:T(8,128)(2,1)S(1)}, bf16[256,1024]{1,0:T(8,128)(2,1)S(1)}, u32[]{:S(2)}, u32[]{:S(2)}) collective-permute-start(bf16[256,1024]{1,0:T(8,128)(2,1)S(1)} %fusion.25), channel_id=1, source_target_pairs={{0,8},{2,10},{4,12},{6,14},{8,0},{10,2},{12,4},{14,6},{1,9},{3,11}... | collective-permute-start | bytes 1572872 | tf_op jit(solution)/shard_map/ppermute | solution.py:17

commit v4 on v3

--- a/solution.py
+++ b/solution.py
@@ -194,13 +194,13 @@
     qkv = jnp.concatenate([qkv_edge, qkv_core], axis=0)
     attended, stats = attend(qkv)
     up_edge_rows = nn(attended[:half], all_out).astype(jnp.bfloat16)
-    update_back = give_back(up_edge_rows)
     update_core = nn(attended[half:], all_out).astype(jnp.bfloat16)
 
     cot_far = after(cot_far, up_edge_rows)
+    update_back = give_back(after(up_edge_rows, cot_far))
     cot_edge = jnp.where(foreign, cot_far, edge(cotangent))
     up = jnp.concatenate([nt(cot_edge, all_out).astype(jnp.bfloat16), up_core], axis=0)
-    grads = reverse(qkv, up, stats)
+    *grads, update_back = lax.optimization_barrier((*reverse(qkv, up, stats), update_back))
 
     def backward(rows, x):
         total = 0.0

time: 122 us -> 117 us (0.959)
  starting transfers between devices: 7.7 us -> 4.82 us
  waiting for transfers between devices: 57.1 us -> 54.9 us
    ppermute x4, starting transfers between devices: 7.11 us -> 4.23 us  [passed_along(): return lax.ppermute(x, 'space', [(i, (i + by) % size) for i in range(size)])]
    ppermute x4, waiting for transfers between devices: 57.1 us -> 54.9 us  [passed_along(): return lax.ppermute(x, 'space', [(i, (i + by) % size) for i in range(size)])]
  transfers between devices with their start and end apart: 6 -> 6, of which waited for: 3 -> 4; matrix products, arithmetic and copies ran while one was open for 16% -> 12% of each run, Pallas kernels for 25% -> 26%
where the time goes in v4:
time: 117 us; the launch traced here: 116 us
  waiting for transfers between devices  54.9 us (47%)
  Pallas kernels  30.3 us (26%)
  matrix products  12.4 us (11%)
  other arithmetic  9.56 us (8%)
  starting transfers between devices  4.82 us (4%)
  local copies, waits for them, and re-layouts  3.06 us (3%)
  between operations  1.52 us (1%)
    ppermute x4, waiting for transfers between devices, passed_along(): return lax.ppermute(x, 'space', [(i, (i + by) % size) for i in range(size)])  54.9 us
    pallas_call x1, Pallas kernels, reverse(): pl.pallas_call(reverse_kernel, grid=(pairs,), in_specs=[cols(0), cols(1),...  18.5 us
    pallas_call x1, Pallas kernels, attend(): pl.pallas_call(attend_kernel, grid=(pairs,), in_specs=[cols(0), cols(1),...  11.8 us
    dot_general x8, matrix products, nt(): lax.dot_general(a, b, (((1,), (1,)), ((), ())), preferred_element_type=jn...  6.37 us
    dot_general x4, matrix products, nn(): lax.dot_general(a, b, (((1,), (0,)), ((), ())), preferred_element_type=jn...  5.99 us
    ppermute x4, starting transfers between devices, passed_along(): return lax.ppermute(x, 'space', [(i, (i + by) % size) for i in range(size)])  4.23 us
    reduce_sum x2, other arithmetic, normalise(): center = values32 - jnp.mean(values32, axis=-1, keepdims=True)  2.63 us
  transfers between devices with their start and end apart: 6, of which 4 were waited for; matrix products, arithmetic and copies ran while one was open for 12% of the time, Pallas kernels for 26%

profile of v4, /device:TPU:0, one launch (start us, length us, event | category | flops | bytes accessed | tf_op | source)
XLA Modules:
  0.0 116.5 jit_solution(17618948433568447553)
XLA Ops:
  0.6 0.5 collective-permute-start.1
  1.1 0.1 collective-permute-start.2
  1.9 1.9 %constant_dynamic-slice_fusion.1 = bf16[256,1024]{1,0:T(8,128)(2,1)} fusion(bf16[512,1024]{1,0:T(8,128)(2,1)} %bitcast.7, s32[]{:T(128)S(6)} %select_n.103), kind=kLoop, calls=%fused_computation.98 | loop fusion | bytes 1048580 | tf_op jit(solution)/shard_map/dynamic_slice | solution.py:147
  3.8 4.0 %collective-permute-start = (bf16[256,1024]{1,0:T(8,128)(2,1)}, bf16[256,1024]{1,0:T(8,128)(2,1)}, u32[]{:S(2)}, u32[]{:S(2)}) collective-permute-start(bf16[256,1024]{1,0:T(8,128)(2,1)} %constant_dynamic-slice_fusion.1), channel_id=1, source_target_pairs={{0,8},{2,10},{4,12},{6,14},{8,0},{10,2},{12,4},{14,6},{1,9},{3,11}... | collective-permute-start | bytes 1572872 | tf_op jit(solution)/shard_map/ppermute | solution.py:17
  7.8 0.0 copy-start.2
  7.8 1.3 %convert_reduce_fusion.1 = f32[256]{0:T(256)S(1)} fusion(bf16[512,1024]{1,0:T(8,128)(2,1)} %bitcast.8, s32[]{:T(128)S(6)} %select_n.104), kind=kLoop, calls=%fused_computation.27 | loop fusion | flops 524032 | bytes 525316 | tf_op jit(solution)/shard_map/reduce_sum | solution.py:128
  9.1 1.3 %fusion.32 = f32[256]{0:T(256)S(1)} fusion(f32[256]{0:T(256)S(1)} %broadcast_multiply_fusion.5, bf16[512,1024]{1,0:T(8,128)(2,1)} %bitcast.9, s32[]{:T(128)S(6)} %select_n.104), kind=kLoop, calls=%fused_computation.53 | loop fusion | flops 1048320 | bytes 526340 | tf_op jit(solution)/shard_map/reduce_sum | solution.py:129
  10.4 0.0 collective-permute-done.2
  10.4 1.7 %broadcast_select_fusion.3 = (bf16[512,1024]{1,0:T(8,128)(2,1)S(1)}, bf16[512,1024]{1,0:T(8,128)(2,1)S(1)}) fusion(bf16[512,1024]{1,0:T(8,128)(2,1)} %param.10, bf16[512,1024]{1,0:T(8,128)(2,1)} %collective-permute-done.2, pred[]{:T(512)S(6)} %eq.3), kind=kLoop, calls=%fused_computation.58 | loop fusion | flops 1048576 | bytes 4194305 | tf_op jit(solution)/shard_map/jit(_where)/select_n | solution.py:174
  12.1 0.0 copy-start.1
  12.1 0.0 copy-done.2
  12.1 0.7 convolution_convert_fusion.3
  12.9 0.0 copy-start
  12.9 0.0 copy-start.3
  12.9 0.0 collective-permute-done.1
  12.9 1.1 copy-done.1
  14.0 0.4 broadcast_select_fusion.1
  14.4 0.1 copy-done
  14.5 0.0 copy-done.3
  14.5 2.2 %fusion.2 = bf16[256,3072]{1,0:T(8,128)(2,1)S(1)} fusion(bf16[512,3072]{1,0:T(8,128)(2,1)S(1)} %get-tuple-element.37, bf16[512,3072]{1,0:T(8,128)(2,1)S(1)} %get-tuple-element.36, f32[1024]{0:T(1024)S(1)} %copy-done.3, f32[256]{0:T(256)S(1)} %add_rsqrt_fusion.1, f32[256]{0:T(256)S(1)} %broadcast_multiply_fusion.5, bf16[512,1024]{1,0:T(8,128)(2,1)S(1)} %bitcast.10, ...), kind=kOutput, calls=%fused_computation.9 | convolution fusion | flops 1625292800 | bytes 8394756 | tf_op jit(solution)/shard_map/dot_general | solution.py:25
  16.7 14.8 %collective-permute-done = bf16[256,1024]{1,0:T(8,128)(2,1)} collective-permute-done((bf16[256,1024]{1,0:T(8,128)(2,1)}, bf16[256,1024]{1,0:T(8,128)(2,1)}, u32[]{:S(2)}, u32[]{:S(2)}) %collective-permute-start) | collective-permute-done | bytes 524320 | tf_op jit(solution)/shard_map/ppermute | solution.py:17
  31.5 1.4 %convert_reduce_fusion = (f32[256]{0:T(256)S(1)}, bf16[256,1024]{1,0:T(8,128)(2,1)S(1)}) fusion(bf16[256,1024]{1,0:T(8,128)(2,1)} %collective-permute-done, pred[256]{0:T(512)(128)(4,1)S(1)} %compare_select_fusion, bf16[512,1024]{1,0:T(8,128)(2,1)S(1)} %bitcast.11, s32[]{:T(128)S(6)} %select_n.103), kind=kLoop, calls=%fused_computation.25 | loop fusion | flops 786176 | bytes 1574148 | tf_op jit(solution)/shard_map/reduce_sum | solution.py:128
  32.9 0.3 fusion.26
  33.2 0.1 collective-permute-start.3
  33.3 2.2 %fusion.3 = bf16[256,3072]{1,0:T(8,128)(2,1)S(1)} fusion(bf16[512,3072]{1,0:T(8,128)(2,1)S(1)} %get-tuple-element.37, bf16[512,3072]{1,0:T(8,128)(2,1)S(1)} %get-tuple-element.36, bf16[256,1024]{1,0:T(8,128)(2,1)S(1)} %get-tuple-element.35, f32[256]{0:T(256)S(1)} %add_rsqrt_fusion, f32[256]{0:T(256)S(1)} %broadcast_multiply_fusion.4, f32[1024]{0:T(1024)S(1)} %copy-done.3), kind=kOutput, calls=%fused_computation.10 | convolution fusion | flops 1625292800 | bytes 8394752 | tf_op jit(solution)/shard_map/dot_general | solution.py:25
  35.5 0.2 pad_maximum_fusion.7.q_ref.k_ref.v_ref
  35.7 11.8 %attend.1 = (bf16[512,1024]{1,0:T(8,128)(2,1)S(1)}, f32[8,4,512]{2,1,0:T(4,128)S(1)}) custom-call(bf16[512,3072]{1,0:T(8,128)(2,1)S(1)} %pad_maximum_fusion.7.q_ref.k_ref.v_ref, bf16[512,3072]{1,0:T(8,128)(2,1)S(1)} %pad_maximum_fusion.7.q_ref.k_ref.v_ref, bf16[512,3072]{1,0:T(8,128)(2,1)S(1)} %pad_maximum_fusion.7.q_ref.k_ref.v_ref), custom_call_target="tpu_custom_call" | custom-call | flops 2147483648 | bytes 4194304 | tf_op jit(solution)/shard_map/attend/pallas_call | solution.py:83
  47.6 0.7 convolution_convert_fusion.1
  48.3 10.5 %collective-permute-done.3 = bf16[256,1024]{1,0:T(8,128)(2,1)S(1)} collective-permute-done((bf16[256,1024]{1,0:T(8,128)(2,1)S(1)}, bf16[256,1024]{1,0:T(8,128)(2,1)S(1)}, u32[]{:S(2)}, u32[]{:S(2)}) %collective-permute-start.3) | collective-permute-done | bytes 524320 | tf_op jit(solution)/shard_map/ppermute | solution.py:17
  58.8 0.7 convolution_convert_fusion
  59.5 0.1 collective-permute-start.4
  59.6 0.1 pad_maximum_fusion.9.up_ref
  59.7 18.5 %reverse.1 = (bf16[512,1024]{1,0:T(8,128)(2,1)S(1)}, bf16[512,1024]{1,0:T(8,128)(2,1)S(1)}, bf16[512,1024]{1,0:T(8,128)(2,1)S(1)}) custom-call(bf16[512,3072]{1,0:T(8,128)(2,1)S(1)} %pad_maximum_fusion.7.q_ref.k_ref.v_ref, bf16[512,3072]{1,0:T(8,128)(2,1)S(1)} %pad_maximum_fusion.7.q_ref.k_ref.v_ref, ...), custom_call_target="tpu_custom_call" | custom-call | flops 5368709120 | bytes 7340032 | tf_op jit(solution)/shard_map/reverse/pallas_call | solution.py:110
  78.2 6.0 %collective-permute-done.4 = bf16[256,1024]{1,0:T(8,128)(2,1)S(1)} collective-permute-done((bf16[256,1024]{1,0:T(8,128)(2,1)S(1)}, bf16[256,1024]{1,0:T(8,128)(2,1)S(1)}, u32[]{:S(2)}, u32[]{:S(2)}) %collective-permute-start.4) | collective-permute-done | bytes 524320 | tf_op jit(solution)/shard_map/ppermute | solution.py:17
  84.1 0.7 fusion.37
  84.9 0.7 fusion.42
  85.6 0.7 fusion.35
  86.4 0.7 fusion.40
  87.1 1.0 fusion.69
  88.1 0.3 fusion.25
  88.5 0.1 collective-permute-start.5
  88.5 1.0 fusion.70
  89.5 23.6 %collective-permute-done.5 = bf16[256,1024]{1,0:T(8,128)(2,1)S(1)} collective-permute-done((bf16[256,1024]{1,0:T(8,128)(2,1)S(1)}, bf16[256,1024]{1,0:T(8,128)(2,1)S(1)}, u32[]{:S(2)}, u32[]{:S(2)}) %collective-permute-start.5) | collective-permute-done | bytes 524320 | tf_op jit(solution)/shard_map/ppermute | solution.py:17
  113.1 0.5 broadcast_select_fusion.8
  113.6 0.8 broadcast_select_fusion.10
  114.4 1.0 pad_maximum_fusion.10
  115.5 1.0 pad_maximum_fusion.11
  (8 shorter events, 0.1 us)
Async XLA Ops:
  0.6 12.3 %collective-permute-start.1 = (bf16[512,3072]{1,0:T(8,128)(2,1)}, bf16[512,3072]{1,0:T(8,128)(2,1)S(1)}, u32[]{:S(2)}, u32[]{:S(2)}) collective-permute-start(bf16[512,3072]{1,0:T(8,128)(2,1)} %param.9), channel_id=1, source_target_pairs={{0,1},{1,0},{2,3},{3,2},{4,5},{5,4},{6,7},{7,6},{8,9},{9,8},{10,11... | collective-permute-start | bytes 9437192 | tf_op jit(solution)/shard_map/ppermute | solution.py:176
  1.1 9.3 %collective-permute-start.2 = (bf16[512,1024]{1,0:T(8,128)(2,1)}, bf16[512,1024]{1,0:T(8,128)(2,1)}, u32[]{:S(2)}, u32[]{:S(2)}) collective-permute-start(bf16[512,1024]{1,0:T(8,128)(2,1)} %param.10), channel_id=1, source_target_pairs={{0,1},{1,0},{2,3},{3,2},{4,5},{5,4},{6,7},{7,6},{8,9},{9,8},{10,11... | collective-permute-start | bytes 3145736 | tf_op jit(solution)/shard_map/ppermute | solution.py:178
  3.8 27.7 %collective-permute-start = (bf16[256,1024]{1,0:T(8,128)(2,1)}, bf16[256,1024]{1,0:T(8,128)(2,1)}, u32[]{:S(2)}, u32[]{:S(2)}) collective-permute-start(bf16[256,1024]{1,0:T(8,128)(2,1)} %constant_dynamic-slice_fusion.1), channel_id=1, source_target_pairs={{0,8},{2,10},{4,12},{6,14},{8,0},{10,2},{12,4},{14,6},{1,9},{3,11}... | collective-permute-start | bytes 1572872 | tf_op jit(solution)/shard_map/ppermute | solution.py:17
  7.8 4.4 %copy-start.2 = (bf16[1,1,8,8,8,1024]{5,4,3,2,1,0:T(8,128)(2,1)S(1)}, bf16[1,1,8,8,8,1024]{5,4,3,2,1,0:T(8,128)(2,1)}, u32[]{:S(2)}) copy-start(bf16[1,1,8,8,8,1024]{5,4,3,2,1,0:T(8,128)(2,1)} %param.7) | copy-start | bytes 3145732
  12.1 1.9 %copy-start.1 = (bf16[512,3072]{1,0:T(8,128)(2,1)S(1)}, bf16[512,3072]{1,0:T(8,128)(2,1)}, u32[]{:S(2)}) copy-start(bf16[512,3072]{1,0:T(8,128)(2,1)} %param.9) | copy-start | bytes 9437188
  12.9 1.6 %copy-start = (bf16[1,1,8,8,8,1024]{5,4,3,2,1,0:T(8,128)(2,1)S(1)}, bf16[1,1,8,8,8,1024]{5,4,3,2,1,0:T(8,128)(2,1)}, u32[]{:S(2)}) copy-start(bf16[1,1,8,8,8,1024]{5,4,3,2,1,0:T(8,128)(2,1)} %param.6) | copy-start | bytes 3145732
  12.9 1.6 %copy-start.3 = (f32[1024]{0:T(1024)S(1)}, f32[1024]{0:T(1024)}, u32[]{:S(2)}) copy-start(f32[1024]{0:T(1024)} %param.11) | copy-start | bytes 12292
  33.2 25.6 %collective-permute-start.3 = (bf16[256,1024]{1,0:T(8,128)(2,1)S(1)}, bf16[256,1024]{1,0:T(8,128)(2,1)S(1)}, u32[]{:S(2)}, u32[]{:S(2)}) collective-permute-start(bf16[256,1024]{1,0:T(8,128)(2,1)S(1)} %constant_dynamic-slice_fusion), channel_id=1, source_target_pairs={{0,8},{2,10},{4,12},{6,14},{8,0},{10,2},{12,4},{14,6},{1,9},{3,11}... | collective-permute-start | bytes 1572872 | tf_op jit(solution)/shard_map/ppermute | solution.py:17
  59.5 24.6 %collective-permute-start.4 = (bf16[256,1024]{1,0:T(8,128)(2,1)S(1)}, bf16[256,1024]{1,0:T(8,128)(2,1)S(1)}, u32[]{:S(2)}, u32[]{:S(2)}) collective-permute-start(bf16[256,1024]{1,0:T(8,128)(2,1)S(1)} %convolution_convert_fusion.1), channel_id=1, source_target_pairs={{0,8},{2,10},{4,12},{6,14},{8,0},{10,2},{12,4},{14,6},{1,9},{3,11}... | collective-permute-start | bytes 1572872 | tf_op jit(solution)/shard_map/ppermute | solution.py:17
  88.5 24.7 %collective-permute-start.5 = (bf16[256,1024]{1,0:T(8,128)(2,1)S(1)}, bf16[256,1024]{1,0:T(8,128)(2,1)S(1)}, u32[]{:S(2)}, u32[]{:S(2)}) collective-permute-start(bf16[256,1024]{1,0:T(8,128)(2,1)S(1)} %fusion.25), channel_id=1, source_target_pairs={{0,8},{2,10},{4,12},{6,14},{8,0},{10,2},{12,4},{14,6},{1,9},{3,11}... | collective-permute-start | bytes 1572872 | tf_op jit(solution)/shard_map/ppermute | solution.py:17

commit v5 on v4

--- a/solution.py
+++ b/solution.py
@@ -1,3 +1,5 @@
+import functools
+
 import jax
 import jax.numpy as jnp
 from jax import lax
@@ -202,7 +204,7 @@
     up = jnp.concatenate([nt(cot_edge, all_out).astype(jnp.bfloat16), up_core], axis=0)
     *grads, update_back = lax.optimization_barrier((*reverse(qkv, up, stats), update_back))
 
-    def backward(rows, x):
+    def backward(rows, x, grads):
         total = 0.0
         for index, piece in enumerate(grads):
             total = total + nt(piece[rows], all_qkv[:, index * channels : (index + 1) * channels])
@@ -212,12 +214,28 @@
         mean_mixed = jnp.mean(grad_normed * normed, axis=-1, keepdims=True)
         return (inverse * (grad_normed - mean_grad - normed * mean_mixed)).astype(jnp.bfloat16)
 
-    grad_edge = backward(slice(0, half), in_edge)
-    grad_back = give_back(grad_edge)
-    grad_core = backward(slice(half, tokens), in_core)
-    update = place(up_edge_rows, update_back, update_core)
-    grad = place(grad_edge, grad_back, grad_core)
-    return update, grad
+    grad_edge = backward(slice(0, half), in_edge, grads)
+    update_back, grad_edge = lax.optimization_barrier((update_back, grad_edge))
+
+    def last(planes, operands):
+        grad_edge, up_edge_rows, update_back, update_core, in_core, *pieces = operands
+        moved = planes * plane
+        offset = jnp.where(upper, half - moved, 0)
+        back = give_back(lax.dynamic_slice_in_dim(grad_edge, offset, moved, 0))
+        grad_core = backward(slice(half, tokens), in_core, pieces)
+        update = place(up_edge_rows, update_back, update_core)
+        back = after(back, grad_core, update)
+        edge_rows = lax.dynamic_update_slice_in_dim(grad_edge, back, offset, 0)
+        low = jnp.where(upper, grad_core, edge_rows)
+        high = jnp.where(upper, edge_rows, grad_core)
+        return update, jnp.concatenate([low, high], axis=0).reshape(tiled_shape)
+
+    travelling = jnp.where(upper, slab - start, start)
+    return lax.switch(
+        travelling - 1,
+        [functools.partial(last, planes) for planes in range(1, slab // 2 + 1)],
+        (grad_edge, up_edge_rows, update_back, update_core, in_core, *grads),
+    )
 
 
 def solution(mesh):

time: 117 us -> 125 us (1.068)
  matrix products: 12.4 us -> 23.3 us
  waiting for transfers between devices: 54.9 us -> 48.3 us
  other arithmetic: 9.56 us -> 12.5 us
    dot_general x8, matrix products: 6.37 us -> 17.4 us  [nt(): lax.dot_general(a, b, (((1,), (1,)), ((), ())), preferred_element_type=jn...]
    ppermute x4, waiting for transfers between devices: 54.9 us -> 48.3 us  [passed_along(): return lax.ppermute(x, 'space', [(i, (i + by) % size) for i in range(size)])]
    concatenate x0 -> x2, other arithmetic: none -> 4.14 us  [the longest x1 3.11 us: whole(): jnp.concatenate([jnp.where(first, own, other), jnp.where(first, other, ow...]
    reduce_sum x2 -> x3, other arithmetic: 2.63 us -> 2.78 us  [normalise(): center = values32 - jnp.mean(values32, axis=-1, keepdims=True)]
  transfers between devices with their start and end apart: 6 -> 6, of which waited for: 4 -> 4; matrix products, arithmetic and copies ran while one was open for 12% -> 18% of each run, Pallas kernels for 26% -> 15%
where the time goes in v5:
time: 125 us; the launch traced here: 124 us
  waiting for transfers between devices  48.3 us (39%)
  Pallas kernels  30.2 us (24%)
  matrix products  23.3 us (19%)
  other arithmetic  12.5 us (10%)
  starting transfers between devices  4.89 us (4%)
  local copies, waits for them, and re-layouts  2.41 us (2%)
  between operations  1.55 us (1%)
    ppermute x4, waiting for transfers between devices, passed_along(): return lax.ppermute(x, 'space', [(i, (i + by) % size) for i in range(size)])  48.3 us
    pallas_call x1, Pallas kernels, reverse(): pl.pallas_call(reverse_kernel, grid=(pairs,), in_specs=[cols(0), cols(1),...  18.5 us
    dot_general x8, matrix products, nt(): lax.dot_general(a, b, (((1,), (1,)), ((), ())), preferred_element_type=jn...  17.4 us
    pallas_call x1, Pallas kernels, attend(): pl.pallas_call(attend_kernel, grid=(pairs,), in_specs=[cols(0), cols(1),...  11.8 us
    dot_general x4, matrix products, nn(): lax.dot_general(a, b, (((1,), (0,)), ((), ())), preferred_element_type=jn...  5.91 us
    ppermute x4, starting transfers between devices, passed_along(): return lax.ppermute(x, 'space', [(i, (i + by) % size) for i in range(size)])  4.29 us
    concatenate x1, other arithmetic, whole(): jnp.concatenate([jnp.where(first, own, other), jnp.where(first, other, ow...  3.11 us
    reduce_sum x3, other arithmetic, normalise(): center = values32 - jnp.mean(values32, axis=-1, keepdims=True)  2.78 us
  transfers between devices with their start and end apart: 6, of which 4 were waited for; matrix products, arithmetic and copies ran while one was open for 18% of the time, Pallas kernels for 15%

profile of v5, /device:TPU:0, one launch (start us, length us, event | category | flops | bytes accessed | tf_op | source)
XLA Modules:
  0.0 123.6 jit_solution(17257452533604794587)
XLA Ops:
  0.6 0.5 collective-permute-start.5
  1.2 0.1 collective-permute-start.6
  1.9 1.1 constant_dynamic-slice_fusion.5
  3.0 4.1 %collective-permute-start.4 = (bf16[256,1024]{1,0:T(8,128)(2,1)S(1)}, bf16[256,1024]{1,0:T(8,128)(2,1)}, u32[]{:S(2)}, u32[]{:S(2)}) collective-permute-start(bf16[256,1024]{1,0:T(8,128)(2,1)S(1)} %constant_dynamic-slice_fusion.5), channel_id=1, source_target_pairs={{0,8},{2,10},{4,12},{6,14},{8,0},{10,2},{12,4},{14,6},{1,9},{3,11}... | collective-permute-start | bytes 1572872 | tf_op jit(solution)/shard_map/ppermute | solution.py:19
  7.1 1.3 %convert_reduce_fusion.5 = (f32[256]{0:T(256)S(1)}, bf16[256,1024]{1,0:T(8,128)(2,1)S(1)}) fusion(bf16[512,1024]{1,0:T(8,128)(2,1)} %bitcast.17, s32[]{:T(128)S(6)} %select_n.205), kind=kLoop, calls=%fused_computation.175 | loop fusion | flops 524032 | bytes 1049604 | tf_op jit(solution)/shard_map/reduce_sum | solution.py:130
  8.4 0.3 fusion.143
  8.7 0.1 broadcast_select_fusion.23
  8.8 0.0 copy-start.3
  8.8 0.0 copy-start.4
  8.9 0.0 copy-start
  8.9 1.6 %convolution_convert_fusion.5 = bf16[256,1024]{1,0:T(8,128)(2,1)} fusion(bf16[512,1024]{1,0:T(8,128)(2,1)S(1)} %bitcast.28, s32[]{:T(128)S(6)} %select_n.205, bf16[512,1024]{1,0:T(8,128)(2,1)S(1)} %get-tuple-element.270, bf16[512,1024]{1,0:T(8,128)(2,1)S(1)} %get-tuple-element.269), kind=kOutput, calls=%fused_computation.179 | convolution fusion | flops 541327360 | bytes 3145732 | tf_op jit(solution)/shard_map/dot_general | solution.py:23
  10.4 1.2 %copy-done = bf16[512,3072]{1,0:T(8,128)(2,1)S(1)} copy-done((bf16[512,3072]{1,0:T(8,128)(2,1)S(1)}, bf16[512,3072]{1,0:T(8,128)(2,1)}, u32[]{:S(2)}) %copy-start) | copy-done | bytes 3145752
  11.7 2.3 %broadcast_select_fusion.21 = (bf16[512,3072]{1,0:T(8,128)(2,1)S(1)}, bf16[512,3072]{1,0:T(8,128)(2,1)S(1)}) fusion(bf16[512,3072]{1,0:T(8,128)(2,1)S(1)} %copy-done, bf16[512,3072]{1,0:T(8,128)(2,1)} %collective-permute-done.5, pred[]{:T(512)S(6)} %eq.3), kind=kLoop, calls=%fused_computation.161 | loop fusion | flops 3145728 | bytes 12582913 | tf_op jit(solution)/shard_map/jit(_where)/select_n | solution.py:176
  14.0 0.0 copy-start.1
  14.0 2.2 %convolution_convert_fusion.1 = bf16[256,3072]{1,0:T(8,128)(2,1)S(1)} fusion(bf16[256,1024]{1,0:T(8,128)(2,1)S(1)} %get-tuple-element.238, f32[1024]{0:T(1024)S(1)} %copy-done.7, f32[256]{0:T(256)S(1)} %add_rsqrt_fusion.5, f32[256]{0:T(256)S(1)} %broadcast_multiply_fusion.15, bf16[512,3072]{1,0:T(8,128)(2,1)S(1)} %get-tuple-element.268, ...), kind=kOutput, calls=%fused_computation.158 | convolution fusion | flops 1625292800 | bytes 8394752 | tf_op jit(solution)/shard_map/dot_general | solution.py:27
  16.3 14.3 %collective-permute-done.4 = bf16[256,1024]{1,0:T(8,128)(2,1)} collective-permute-done((bf16[256,1024]{1,0:T(8,128)(2,1)S(1)}, bf16[256,1024]{1,0:T(8,128)(2,1)}, u32[]{:S(2)}, u32[]{:S(2)}) %collective-permute-start.4) | collective-permute-done | bytes 524320 | tf_op jit(solution)/shard_map/ppermute | solution.py:19
  30.6 1.3 %convert_reduce_fusion.4 = (f32[256]{0:T(256)S(1)}, bf16[256,1024]{1,0:T(8,128)(2,1)S(1)}) fusion(bf16[256,1024]{1,0:T(8,128)(2,1)} %collective-permute-done.4, pred[256]{0:T(512)(128)(4,1)S(1)} %compare_select_fusion.4, bf16[512,1024]{1,0:T(8,128)(2,1)S(1)} %bitcast.18, s32[]{:T(128)S(6)} %select_n.204), kind=kLoop, calls=%fused_computation.173 | loop fusion | flops 786176 | bytes 1574148 | tf_op jit(solution)/shard_map/reduce_sum | solution.py:130
  31.9 0.3 fusion.142
  32.2 2.2 %convolution_convert_fusion = bf16[256,3072]{1,0:T(8,128)(2,1)S(1)} fusion(bf16[256,1024]{1,0:T(8,128)(2,1)S(1)} %get-tuple-element.236, f32[256]{0:T(256)S(1)} %add_rsqrt_fusion.4, f32[256]{0:T(256)S(1)} %broadcast_multiply_fusion.14, f32[1024]{0:T(1024)S(1)} %copy-done.7, bf16[512,3072]{1,0:T(8,128)(2,1)S(1)} %get-tuple-element.268, ...), kind=kOutput, calls=%fused_computation.157 | convolution fusion | flops 1625292800 | bytes 8394752 | tf_op jit(solution)/shard_map/dot_general | solution.py:27
  34.5 0.2 pad_maximum_fusion.9.q_ref.k_ref.v_ref
  34.7 11.8 %attend.1 = (bf16[512,1024]{1,0:T(8,128)(2,1)S(1)}, f32[8,4,512]{2,1,0:T(4,128)S(1)}) custom-call(bf16[512,3072]{1,0:T(8,128)(2,1)S(1)} %pad_maximum_fusion.9.q_ref.k_ref.v_ref, bf16[512,3072]{1,0:T(8,128)(2,1)S(1)} %pad_maximum_fusion.9.q_ref.k_ref.v_ref, bf16[512,3072]{1,0:T(8,128)(2,1)S(1)} %pad_maximum_fusion.9.q_ref.k_ref.v_ref), custom_call_target="tpu_custom_call" | custom-call | flops 2147483648 | bytes 4194304 | tf_op jit(solution)/shard_map/attend/pallas_call | solution.py:85
  46.5 0.7 convolution_convert_fusion.4
  47.3 0.1 collective-permute-start.7
  47.4 0.7 convolution_convert_fusion.2
  48.1 3.1 %pad_maximum_fusion.8 = bf16[1024,3072]{1,0:T(8,128)(2,1)} fusion(bf16[512,3072]{1,0:T(8,128)(2,1)S(1)} %get-tuple-element.268, bf16[512,3072]{1,0:T(8,128)(2,1)S(1)} %get-tuple-element.267), kind=kLoop, calls=%fused_computation.153 | loop fusion | flops 12582912 | bytes 12582912 | tf_op jit(solution)/shard_map/concatenate | solution.py:176
  51.2 21.7 %collective-permute-done.7 = bf16[256,1024]{1,0:T(8,128)(2,1)S(1)} collective-permute-done((bf16[256,1024]{1,0:T(8,128)(2,1)S(1)}, bf16[256,1024]{1,0:T(8,128)(2,1)S(1)}, u32[]{:S(2)}, u32[]{:S(2)}) %collective-permute-start.7) | collective-permute-done | bytes 524320 | tf_op jit(solution)/shard_map/ppermute | solution.py:19
  72.9 2.5 %convolution_convert_fusion.3 = bf16[256,1024]{1,0:T(8,128)(2,1)S(1)} fusion(bf16[256,1024]{1,0:T(8,128)(2,1)S(1)} %collective-permute-done.7, bf16[512,1024]{1,0:T(8,128)(2,1)} %bitcast.27, s32[]{:T(128)S(6)} %select_n.204, pred[256]{0:T(512)(128)(4,1)S(1)} %compare_select_fusion.4, bf16[512,1024]{1,0:T(8,128)(2,1)} %copy-done.4, ...), kind=kOutput, calls=%fused_computation.177 | convolution fusion | flops 541589504 | bytes 3670276 | tf_op jit(solution)/shard_map/dot_general | solution.py:23
  75.3 0.1 collective-permute-start.8
  75.4 0.1 pad_maximum_fusion.11.up_ref
  75.5 18.5 %reverse.1 = (bf16[512,1024]{1,0:T(8,128)(2,1)}, bf16[512,1024]{1,0:T(8,128)(2,1)}, bf16[512,1024]{1,0:T(8,128)(2,1)}) custom-call(bf16[512,3072]{1,0:T(8,128)(2,1)S(1)} %pad_maximum_fusion.9.q_ref.k_ref.v_ref, bf16[512,3072]{1,0:T(8,128)(2,1)S(1)} %pad_maximum_fusion.9.q_ref.k_ref.v_ref, bf16[512,3072]{1,0:T(8,128)(2,1)S(1)} %pad_maximum_fusion.9.q_ref.k_ref.v_ref, ...), custom_call_target="tpu_custom_call" | custom-call | flops 5368709120 | bytes 7340032 | tf_op jit(solution)/shard_map/reverse/pallas_call | solution.py:112
  94.0 6.0 %collective-permute-done.8 = bf16[256,1024]{1,0:T(8,128)(2,1)S(1)} collective-permute-done((bf16[256,1024]{1,0:T(8,128)(2,1)S(1)}, bf16[256,1024]{1,0:T(8,128)(2,1)S(1)}, u32[]{:S(2)}, u32[]{:S(2)}) %collective-permute-start.8) | collective-permute-done | bytes 524320 | tf_op jit(solution)/shard_map/ppermute | solution.py:19
  99.9 1.8 %fusion.117 = f32[256,1024]{1,0:T(8,128)S(1)} fusion(bf16[512,3072]{1,0:T(8,128)(2,1)S(1)} %get-tuple-element.267, bf16[512,3072]{1,0:T(8,128)(2,1)S(1)} %get-tuple-element.268, bf16[512,1024]{1,0:T(8,128)(2,1)} %get-tuple-element.176), kind=kOutput, calls=%fused_computation.167 | convolution fusion | flops 541065216 | bytes 7864320 | tf_op jit(solution)/shard_map/dot_general | solution.py:23
  101.7 1.8 %fusion.115 = f32[256,1024]{1,0:T(8,128)S(1)} fusion(bf16[512,3072]{1,0:T(8,128)(2,1)S(1)} %get-tuple-element.267, bf16[512,3072]{1,0:T(8,128)(2,1)S(1)} %get-tuple-element.268, bf16[512,1024]{1,0:T(8,128)(2,1)} %get-tuple-element.177), kind=kOutput, calls=%fused_computation.166 | convolution fusion | flops 541065216 | bytes 7864320 | tf_op jit(solution)/shard_map/dot_general | solution.py:23
  103.5 2.1 %fusion.172 = (f32[256]{0:T(256)S(1)}, f32[256]{0:T(256)S(1)}, f32[256,1024]{1,0:T(8,128)S(1)}) fusion(f32[256]{0:T(256)S(1)} %add_rsqrt_fusion.4, f32[256]{0:T(256)S(1)} %broadcast_multiply_fusion.14, bf16[256,1024]{1,0:T(8,128)(2,1)S(1)} %get-tuple-element.236, f32[1024]{0:T(1024)S(1)} %copy-done.7, f32[256,1024]{1,0:T(8,128)S(1)} %fusion.115, ...), kind=kOutput, calls=%fused_computation.242 | convolution fusion | flops 543424000 | bytes 10493952 | tf_op jit(solution)/shard_map/dot_general | solution.py:23
  105.6 0.3 fusion.141
  105.9 17.7 %conditional.1 = (bf16[1,1,8,8,8,1024]{5,4,3,2,1,0:T(8,128)(2,1)}, bf16[1,1,8,8,8,1024]{5,4,3,2,1,0:T(8,128)(2,1)}) conditional(s32[]{:T(128)} %clamp.3, (pred[]{:T(512)}, pred[]{:T(512)}, bf16[256,1024]{1,0:T(8,128)(2,1)S(1)}, bf16[256,1024]{1,0:T(8,128)(2,1)S(1)}, bf16[256,1024]{1,0:T(8,128)(2,1)S(1)}, ...), branch_computations={%region_6.11_spmd, %region_11.16_spmd, %region_16.21_spmd, %region... | conditional | flops 1622148352 | bytes 28863060 | solution.py:234
  106.2 0.1 collective-permute-start.3
  106.3 0.1 convert_reduce_fusion.3
  106.5 0.3 fusion.107
  106.8 2.5 %fusion.84 = f32[256,1024]{1,0:T(8,128)S(1)} fusion(bf16[1024,3072]{1,0:T(8,128)(2,1)} %get-tuple-element.142, bf16[512,1024]{1,0:T(8,128)(2,1)} %get-tuple-element.144), kind=kOutput, calls=%fused_computation.114 | convolution fusion | flops 536870912 | bytes 3670016 | tf_op jit(solution)/shard_map/cond/branch_3_fun/dot_general | solution.py:23
  109.3 2.5 %fusion.86 = f32[256,1024]{1,0:T(8,128)S(1)} fusion(bf16[1024,3072]{1,0:T(8,128)(2,1)} %get-tuple-element.142, bf16[512,1024]{1,0:T(8,128)(2,1)} %get-tuple-element.143), kind=kOutput, calls=%fused_computation.116 | convolution fusion | flops 536870912 | bytes 3670016 | tf_op jit(solution)/shard_map/cond/branch_3_fun/dot_general | solution.py:23
  111.8 2.8 %fusion.171 = (f32[256]{0:T(256)S(1)}, f32[256]{0:T(256)S(1)}, f32[256,1024]{1,0:T(8,128)S(1)}) fusion(f32[256]{0:T(256)S(1)} %add_rsqrt_fusion.3, f32[256]{0:T(256)S(1)} %broadcast_multiply_fusion.11, bf16[256,1024]{1,0:T(8,128)(2,1)S(1)} %get-tuple-element.140, f32[1024]{0:T(1024)S(1)} %get-tuple-element.145, f32[256,1024]{1,0:T(8,128)S(1)} %fusion.84, ...), kind=kOutput, calls=%fused_computation.241 | convolution fusion | flops 539229696 | bytes 6299648 | tf_op jit(solution)/shard_map/cond/branch_3_fun/dot_general | solution.py:23
  114.6 0.2 broadcast_select_fusion.19
  114.8 1.0 pad_maximum_fusion.6
  115.8 0.3 fusion.106
  116.1 6.4 %collective-permute-done.3 = bf16[256,1024]{1,0:T(8,128)(2,1)S(1)} collective-permute-done((bf16[256,1024]{1,0:T(8,128)(2,1)S(1)}, bf16[256,1024]{1,0:T(8,128)(2,1)S(1)}, u32[]{:S(2)}, u32[]{:S(2)}) %collective-permute-start.3) | collective-permute-done | bytes 524320 | tf_op jit(solution)/shard_map/cond/branch_3_fun/ppermute | solution.py:19
  122.5 0.1 broadcast_select_fusion.17
  122.6 1.0 pad_maximum_fusion.7
  (26 shorter events, 0.2 us)
Async XLA Ops:
  0.6 8.0 %copy-start.2 = (bf16[512,1024]{1,0:T(8,128)(2,1)S(1)}, bf16[512,1024]{1,0:T(8,128)(2,1)}, u32[]{:S(2)}) copy-start(bf16[512,1024]{1,0:T(8,128)(2,1)} %param.14) | copy-start | bytes 3145732
  0.6 9.8 %collective-permute-start.5 = (bf16[512,3072]{1,0:T(8,128)(2,1)}, bf16[512,3072]{1,0:T(8,128)(2,1)}, u32[]{:S(2)}, u32[]{:S(2)}) collective-permute-start(bf16[512,3072]{1,0:T(8,128)(2,1)} %param.13), channel_id=1, source_target_pairs={{0,1},{1,0},{2,3},{3,2},{4,5},{5,4},{6,7},{7,6},{8,9},{9,8},{10,11... | collective-permute-start | bytes 9437192 | tf_op jit(solution)/shard_map/ppermute | solution.py:178
  1.2 7.5 %collective-permute-start.6 = (bf16[512,1024]{1,0:T(8,128)(2,1)}, bf16[512,1024]{1,0:T(8,128)(2,1)S(1)}, u32[]{:S(2)}, u32[]{:S(2)}) collective-permute-start(bf16[512,1024]{1,0:T(8,128)(2,1)} %param.14), channel_id=1, source_target_pairs={{0,1},{1,0},{2,3},{3,2},{4,5},{5,4},{6,7},{7,6},{8,9},{9,8},{10,11... | collective-permute-start | bytes 3145736 | tf_op jit(solution)/shard_map/ppermute | solution.py:180
  3.0 27.6 %collective-permute-start.4 = (bf16[256,1024]{1,0:T(8,128)(2,1)S(1)}, bf16[256,1024]{1,0:T(8,128)(2,1)}, u32[]{:S(2)}, u32[]{:S(2)}) collective-permute-start(bf16[256,1024]{1,0:T(8,128)(2,1)S(1)} %constant_dynamic-slice_fusion.5), channel_id=1, source_target_pairs={{0,8},{2,10},{4,12},{6,14},{8,0},{10,2},{12,4},{14,6},{1,9},{3,11}... | collective-permute-start | bytes 1572872 | tf_op jit(solution)/shard_map/ppermute | solution.py:19
  7.1 1.8 %copy-start.6 = (bf16[1,1,8,8,8,1024]{5,4,3,2,1,0:T(8,128)(2,1)S(1)}, bf16[1,1,8,8,8,1024]{5,4,3,2,1,0:T(8,128)(2,1)}, u32[]{:S(2)}) copy-start(bf16[1,1,8,8,8,1024]{5,4,3,2,1,0:T(8,128)(2,1)} %param.11) | copy-start | bytes 3145732
  8.8 38.5 %copy-start.3 = (bf16[512,1024]{1,0:T(8,128)(2,1)}, bf16[512,1024]{1,0:T(8,128)(2,1)S(1)}, u32[]{:S(2)}) copy-start(bf16[512,1024]{1,0:T(8,128)(2,1)S(1)} %get-tuple-element.269) | copy-start | bytes 3145732
  8.8 38.5 %copy-start.4 = (bf16[512,1024]{1,0:T(8,128)(2,1)}, bf16[512,1024]{1,0:T(8,128)(2,1)S(1)}, u32[]{:S(2)}) copy-start(bf16[512,1024]{1,0:T(8,128)(2,1)S(1)} %get-tuple-element.270) | copy-start | bytes 3145732
  8.9 2.8 %copy-start = (bf16[512,3072]{1,0:T(8,128)(2,1)S(1)}, bf16[512,3072]{1,0:T(8,128)(2,1)}, u32[]{:S(2)}) copy-start(bf16[512,3072]{1,0:T(8,128)(2,1)} %param.13) | copy-start | bytes 9437188
  10.4 3.6 %copy-start.7 = (f32[1024]{0:T(1024)S(1)}, f32[1024]{0:T(1024)}, u32[]{:S(2)}) copy-start(f32[1024]{0:T(1024)} %param.15) | copy-start | bytes 12292
  14.0 16.6 %copy-start.1 = (bf16[1,1,8,8,8,1024]{5,4,3,2,1,0:T(8,128)(2,1)S(1)}, bf16[1,1,8,8,8,1024]{5,4,3,2,1,0:T(8,128)(2,1)}, u32[]{:S(2)}) copy-start(bf16[1,1,8,8,8,1024]{5,4,3,2,1,0:T(8,128)(2,1)} %param.10) | copy-start | bytes 3145732
  47.3 25.6 %collective-permute-start.7 = (bf16[256,1024]{1,0:T(8,128)(2,1)S(1)}, bf16[256,1024]{1,0:T(8,128)(2,1)S(1)}, u32[]{:S(2)}, u32[]{:S(2)}) collective-permute-start(bf16[256,1024]{1,0:T(8,128)(2,1)S(1)} %constant_dynamic-slice_fusion.3), channel_id=1, source_target_pairs={{0,8},{2,10},{4,12},{6,14},{8,0},{10,2},{12,4},{14,6},{1,9},{3,11}... | collective-permute-start | bytes 1572872 | tf_op jit(solution)/shard_map/ppermute | solution.py:19
  51.2 24.2 %copy-start.5 = (bf16[256,1024]{1,0:T(8,128)(2,1)S(1)}, bf16[256,1024]{1,0:T(8,128)(2,1)}, u32[]{:S(2)}) copy-start(bf16[256,1024]{1,0:T(8,128)(2,1)} %convolution_convert_fusion.5) | copy-start | bytes 1572868
  75.3 24.6 %collective-permute-start.8 = (bf16[256,1024]{1,0:T(8,128)(2,1)S(1)}, bf16[256,1024]{1,0:T(8,128)(2,1)S(1)}, u32[]{:S(2)}, u32[]{:S(2)}) collective-permute-start(bf16[256,1024]{1,0:T(8,128)(2,1)S(1)} %convolution_convert_fusion.4), channel_id=1, source_target_pairs={{0,8},{2,10},{4,12},{6,14},{8,0},{10,2},{12,4},{14,6},{1,9},{3,11}... | collective-permute-start | bytes 1572872 | tf_op jit(solution)/shard_map/ppermute | solution.py:19
  106.2 16.3 %collective-permute-start.3 = (bf16[256,1024]{1,0:T(8,128)(2,1)S(1)}, bf16[256,1024]{1,0:T(8,128)(2,1)S(1)}, u32[]{:S(2)}, u32[]{:S(2)}) collective-permute-start(bf16[256,1024]{1,0:T(8,128)(2,1)S(1)} %get-tuple-element.146), channel_id=1, source_target_pairs={{0,8},{2,10},{4,12},{6,14},{8,0},{10,2},{12,4},{14,6},{1,9},{3,11}... | collective-permute-start | bytes 1572872 | tf_op jit(solution)/shard_map/cond/branch_3_fun/ppermute | solution.py:19

commit v6 on v5

--- a/solution.py
+++ b/solution.py
@@ -195,11 +195,11 @@
     qkv_edge = project(in_edge)
     qkv = jnp.concatenate([qkv_edge, qkv_core], axis=0)
     attended, stats = attend(qkv)
+    attended, stats, cot_far = lax.optimization_barrier((attended, stats, cot_far))
     up_edge_rows = nn(attended[:half], all_out).astype(jnp.bfloat16)
     update_core = nn(attended[half:], all_out).astype(jnp.bfloat16)
 
-    cot_far = after(cot_far, up_edge_rows)
-    update_back = give_back(after(up_edge_rows, cot_far))
+    update_back = give_back(up_edge_rows)
     cot_edge = jnp.where(foreign, cot_far, edge(cotangent))
     up = jnp.concatenate([nt(cot_edge, all_out).astype(jnp.bfloat16), up_core], axis=0)
     *grads, update_back = lax.optimization_barrier((*reverse(qkv, up, stats), update_back))

time: 125 us -> 114 us (0.912); the launches traced: 124 us -> 114 us
  waiting for transfers between devices: 48.3 us -> 37.1 us
  local copies, waits for them, and re-layouts: 2.41 us -> 5.33 us
    ppermute x4, waiting for transfers between devices: 48.3 us -> 37.1 us  [passed_along(): return lax.ppermute(x, 'space', [(i, (i + by) % size) for i in range(size)])]
    unnamed x16 -> x30, local copies, waits for them, and re-layouts: 1.29 us -> 3.42 us
    dot_general x8, matrix products: 17.4 us -> 15.8 us  [nt(): lax.dot_general(a, b, (((1,), (1,)), ((), ())), preferred_element_type=jn...]
    dot_general x4, matrix products: 5.91 us -> 7.47 us  [nn(): lax.dot_general(a, b, (((1,), (0,)), ((), ())), preferred_element_type=jn...]
  transfers between devices with their start and end apart: 6 -> 6, of which waited for: 4 -> 4; matrix products, arithmetic and copies ran while one was open for 18% -> 20% of each run, Pallas kernels for 15% -> 27%
where the time goes in v6:
time: 114 us
  waiting for transfers between devices  37.1 us (33%)
  Pallas kernels  30.2 us (26%)
  matrix products  23.2 us (20%)
  other arithmetic  11.5 us (10%)
  local copies, waits for them, and re-layouts  5.33 us (5%)
  starting transfers between devices  4.82 us (4%)
  between operations  1.6 us (1%)
    ppermute x4, waiting for transfers between devices, passed_along(): return lax.ppermute(x, 'space', [(i, (i + by) % size) for i in range(size)])  37.1 us
    pallas_call x1, Pallas kernels, reverse(): pl.pallas_call(reverse_kernel, grid=(pairs,), in_specs=[cols(0), cols(1),...  18.4 us
    dot_general x8, matrix products, nt(): lax.dot_general(a, b, (((1,), (1,)), ((), ())), preferred_element_type=jn...  15.8 us
    pallas_call x1, Pallas kernels, attend(): pl.pallas_call(attend_kernel, grid=(pairs,), in_specs=[cols(0), cols(1),...  11.8 us
    dot_general x4, matrix products, nn(): lax.dot_general(a, b, (((1,), (0,)), ((), ())), preferred_element_type=jn...  7.47 us
    ppermute x4, starting transfers between devices, passed_along(): return lax.ppermute(x, 'space', [(i, (i + by) % size) for i in range(size)])  4.23 us
    unnamed x30, local copies, waits for them, and re-layouts  3.42 us
    concatenate x1, other arithmetic, whole(): jnp.concatenate([jnp.where(first, own, other), jnp.where(first, other, ow...  3.11 us
  transfers between devices with their start and end apart: 6, of which 4 were waited for; matrix products, arithmetic and copies ran while one was open for 20% of the time, Pallas kernels for 27%

profile of v6, /device:TPU:0, one launch (start us, length us, event | category | flops | bytes accessed | tf_op | source)
XLA Modules:
  0.0 114.1 jit_solution(16027909544072383047)
XLA Ops:
  0.6 0.5 collective-permute-start.5
  1.2 0.1 collective-permute-start.6
  1.9 1.9 %constant_dynamic-slice_fusion.5 = bf16[256,1024]{1,0:T(8,128)(2,1)} fusion(bf16[512,1024]{1,0:T(8,128)(2,1)} %bitcast.16, s32[]{:T(128)S(6)} %select_n.204), kind=kLoop, calls=%fused_computation.228 | loop fusion | bytes 1048580 | tf_op jit(solution)/shard_map/dynamic_slice | solution.py:149
  3.8 4.0 %collective-permute-start.4 = (bf16[256,1024]{1,0:T(8,128)(2,1)}, bf16[256,1024]{1,0:T(8,128)(2,1)S(1)}, u32[]{:S(2)}, u32[]{:S(2)}) collective-permute-start(bf16[256,1024]{1,0:T(8,128)(2,1)} %constant_dynamic-slice_fusion.5), channel_id=1, source_target_pairs={{0,8},{2,10},{4,12},{6,14},{8,0},{10,2},{12,4},{14,6},{1,9},{3,11}... | collective-permute-start | bytes 1572872 | tf_op jit(solution)/shard_map/ppermute | solution.py:19
  7.8 1.3 %convert_reduce_fusion.5 = (f32[256]{0:T(256)S(1)}, bf16[256,1024]{1,0:T(8,128)(2,1)S(1)}) fusion(bf16[512,1024]{1,0:T(8,128)(2,1)} %bitcast.17, s32[]{:T(128)S(6)} %select_n.205), kind=kLoop, calls=%fused_computation.175 | loop fusion | flops 524032 | bytes 1049604 | tf_op jit(solution)/shard_map/reduce_sum | solution.py:130
  9.1 0.3 fusion.143
  9.4 0.1 broadcast_select_fusion.23
  9.6 1.6 %convolution_convert_fusion.5 = bf16[256,1024]{1,0:T(8,128)(2,1)} fusion(bf16[512,1024]{1,0:T(8,128)(2,1)S(1)} %bitcast.27, s32[]{:T(128)S(6)} %select_n.205, bf16[512,1024]{1,0:T(8,128)(2,1)S(1)} %get-tuple-element.272, bf16[512,1024]{1,0:T(8,128)(2,1)S(1)} %get-tuple-element.271), kind=kOutput, calls=%fused_computation.179 | convolution fusion | flops 541327360 | bytes 3145732 | tf_op jit(solution)/shard_map/dot_general | solution.py:23
  11.2 1.2 %copy-done.2 = bf16[512,3072]{1,0:T(8,128)(2,1)S(1)} copy-done((bf16[512,3072]{1,0:T(8,128)(2,1)S(1)}, bf16[512,3072]{1,0:T(8,128)(2,1)}, u32[]{:S(2)}) %copy-start.2) | copy-done | bytes 3145752
  12.4 2.3 %broadcast_select_fusion.21 = (bf16[512,3072]{1,0:T(8,128)(2,1)S(1)}, bf16[512,3072]{1,0:T(8,128)(2,1)S(1)}) fusion(bf16[512,3072]{1,0:T(8,128)(2,1)S(1)} %copy-done.2, bf16[512,3072]{1,0:T(8,128)(2,1)} %collective-permute-done.5, pred[]{:T(512)S(6)} %eq.3), kind=kLoop, calls=%fused_computation.161 | loop fusion | flops 3145728 | bytes 12582913 | tf_op jit(solution)/shard_map/jit(_where)/select_n | solution.py:176
  14.8 2.3 %convolution_convert_fusion.1 = bf16[256,3072]{1,0:T(8,128)(2,1)S(1)} fusion(bf16[256,1024]{1,0:T(8,128)(2,1)S(1)} %get-tuple-element.240, f32[1024]{0:T(1024)S(1)} %copy-done.12, f32[256]{0:T(256)S(1)} %add_rsqrt_fusion.5, f32[256]{0:T(256)S(1)} %broadcast_multiply_fusion.15, bf16[512,3072]{1,0:T(8,128)(2,1)S(1)} %get-tuple-element.270, ...), kind=kOutput, calls=%fused_computation.158 | convolution fusion | flops 1625292800 | bytes 8394752 | tf_op jit(solution)/shard_map/dot_general | solution.py:27
  17.0 14.4 %collective-permute-done.4 = bf16[256,1024]{1,0:T(8,128)(2,1)S(1)} collective-permute-done((bf16[256,1024]{1,0:T(8,128)(2,1)}, bf16[256,1024]{1,0:T(8,128)(2,1)S(1)}, u32[]{:S(2)}, u32[]{:S(2)}) %collective-permute-start.4) | collective-permute-done | bytes 524320 | tf_op jit(solution)/shard_map/ppermute | solution.py:19
  31.4 0.3 convert_reduce_fusion.4
  31.7 0.3 fusion.142
  32.0 0.5 copy-done
  32.5 2.2 %convolution_convert_fusion = bf16[256,3072]{1,0:T(8,128)(2,1)S(1)} fusion(bf16[256,1024]{1,0:T(8,128)(2,1)S(1)} %get-tuple-element.238, f32[256]{0:T(256)S(1)} %add_rsqrt_fusion.4, f32[256]{0:T(256)S(1)} %broadcast_multiply_fusion.14, f32[1024]{0:T(1024)S(1)} %copy-done.12, bf16[512,3072]{1,0:T(8,128)(2,1)S(1)} %get-tuple-element.270, ...), kind=kOutput, calls=%fused_computation.157 | convolution fusion | flops 1625292800 | bytes 8394752 | tf_op jit(solution)/shard_map/dot_general | solution.py:27
  34.8 0.2 pad_maximum_fusion.9.q_ref.k_ref.v_ref
  35.0 0.1 collective-permute-start.7
  35.1 11.8 %attend.1 = (bf16[512,1024]{1,0:T(8,128)(2,1)S(1)}, f32[8,4,512]{2,1,0:T(4,128)S(1)}) custom-call(bf16[512,3072]{1,0:T(8,128)(2,1)S(1)} %pad_maximum_fusion.9.q_ref.k_ref.v_ref, bf16[512,3072]{1,0:T(8,128)(2,1)S(1)} %pad_maximum_fusion.9.q_ref.k_ref.v_ref, bf16[512,3072]{1,0:T(8,128)(2,1)S(1)} %pad_maximum_fusion.9.q_ref.k_ref.v_ref), custom_call_target="tpu_custom_call" | custom-call | flops 2147483648 | bytes 4194304 | tf_op jit(solution)/shard_map/attend/pallas_call | solution.py:85
  46.9 3.1 %pad_maximum_fusion.8 = bf16[1024,3072]{1,0:T(8,128)(2,1)} fusion(bf16[512,3072]{1,0:T(8,128)(2,1)S(1)} %get-tuple-element.270, bf16[512,3072]{1,0:T(8,128)(2,1)S(1)} %get-tuple-element.269), kind=kLoop, calls=%fused_computation.153 | loop fusion | flops 12582912 | bytes 12582912 | tf_op jit(solution)/shard_map/concatenate | solution.py:176
  50.0 10.6 %collective-permute-done.7 = bf16[256,1024]{1,0:T(8,128)(2,1)S(1)} collective-permute-done((bf16[256,1024]{1,0:T(8,128)(2,1)S(1)}, bf16[256,1024]{1,0:T(8,128)(2,1)S(1)}, u32[]{:S(2)}, u32[]{:S(2)}) %collective-permute-start.7) | collective-permute-done | bytes 524320 | tf_op jit(solution)/shard_map/ppermute | solution.py:19
  60.6 0.8 copy-done.13
  61.4 2.2 %convolution_convert_fusion.3 = bf16[256,1024]{1,0:T(8,128)(2,1)S(1)} fusion(bf16[512,1024]{1,0:T(8,128)(2,1)S(1)} %get-tuple-element.175, bf16[512,1024]{1,0:T(8,128)(2,1)} %copy-done.7, bf16[512,1024]{1,0:T(8,128)(2,1)} %copy-done.5), kind=kOutput, calls=%fused_computation.177 | convolution fusion | flops 541327360 | bytes 3145728 | tf_op jit(solution)/shard_map/dot_general | solution.py:27
  63.7 0.7 convolution_convert_fusion.2
  64.5 0.5 copy-done.11
  64.9 0.1 copy-done.14
  65.1 0.8 convolution_convert_fusion.4
  65.8 0.1 collective-permute-start.8
  65.9 0.2 copy-done.9
  66.2 18.4 %reverse.1 = (bf16[512,1024]{1,0:T(8,128)(2,1)}, bf16[512,1024]{1,0:T(8,128)(2,1)}, bf16[512,1024]{1,0:T(8,128)(2,1)}) custom-call(bf16[512,3072]{1,0:T(8,128)(2,1)S(1)} %pad_maximum_fusion.9.q_ref.k_ref.v_ref, bf16[512,3072]{1,0:T(8,128)(2,1)S(1)} %pad_maximum_fusion.9.q_ref.k_ref.v_ref, bf16[512,3072]{1,0:T(8,128)(2,1)S(1)} %pad_maximum_fusion.9.q_ref.k_ref.v_ref, ...), custom_call_target="tpu_custom_call" | custom-call | flops 5368709120 | bytes 7340032 | tf_op jit(solution)/shard_map/reverse/pallas_call | solution.py:112
  84.6 5.8 %collective-permute-done.8 = bf16[256,1024]{1,0:T(8,128)(2,1)S(1)} collective-permute-done((bf16[256,1024]{1,0:T(8,128)(2,1)S(1)}, bf16[256,1024]{1,0:T(8,128)(2,1)S(1)}, u32[]{:S(2)}, u32[]{:S(2)}) %collective-permute-start.8) | collective-permute-done | bytes 524320 | tf_op jit(solution)/shard_map/ppermute | solution.py:19
  90.4 1.8 %fusion.115 = f32[256,1024]{1,0:T(8,128)S(1)} fusion(bf16[512,3072]{1,0:T(8,128)(2,1)S(1)} %get-tuple-element.269, bf16[512,3072]{1,0:T(8,128)(2,1)S(1)} %get-tuple-element.270, bf16[512,1024]{1,0:T(8,128)(2,1)} %get-tuple-element.179), kind=kOutput, calls=%fused_computation.166 | convolution fusion | flops 541065216 | bytes 7864320 | tf_op jit(solution)/shard_map/dot_general | solution.py:23
  92.2 1.8 %fusion.117 = f32[256,1024]{1,0:T(8,128)S(1)} fusion(bf16[512,3072]{1,0:T(8,128)(2,1)S(1)} %get-tuple-element.269, bf16[512,3072]{1,0:T(8,128)(2,1)S(1)} %get-tuple-element.270, bf16[512,1024]{1,0:T(8,128)(2,1)} %get-tuple-element.178), kind=kOutput, calls=%fused_computation.167 | convolution fusion | flops 541065216 | bytes 7864320 | tf_op jit(solution)/shard_map/dot_general | solution.py:23
  94.1 2.0 %fusion.172 = (f32[256]{0:T(256)S(1)}, f32[256]{0:T(256)S(1)}, f32[256,1024]{1,0:T(8,128)S(1)}) fusion(f32[256]{0:T(256)S(1)} %add_rsqrt_fusion.4, f32[256]{0:T(256)S(1)} %broadcast_multiply_fusion.14, bf16[256,1024]{1,0:T(8,128)(2,1)S(1)} %copy-done.1, f32[1024]{0:T(1024)S(1)} %copy-done.12, f32[256,1024]{1,0:T(8,128)S(1)} %fusion.115, ...), kind=kOutput, calls=%fused_computation.242 | convolution fusion | flops 543424000 | bytes 10493952 | tf_op jit(solution)/shard_map/dot_general | solution.py:23
  96.2 0.3 fusion.141
  96.5 17.6 %conditional.1 = (bf16[1,1,8,8,8,1024]{5,4,3,2,1,0:T(8,128)(2,1)}, bf16[1,1,8,8,8,1024]{5,4,3,2,1,0:T(8,128)(2,1)}) conditional(s32[]{:T(128)} %clamp.3, (pred[]{:T(512)}, pred[]{:T(512)}, bf16[256,1024]{1,0:T(8,128)(2,1)S(1)}, bf16[256,1024]{1,0:T(8,128)(2,1)S(1)}, bf16[256,1024]{1,0:T(8,128)(2,1)S(1)}, ...), branch_computations={%region_6.11_spmd, %region_11.16_spmd, %region_16.21_spmd, %region... | conditional | flops 1622148352 | bytes 28863060 | solution.py:234
  96.8 0.1 collective-permute-start.3
  96.9 0.1 convert_reduce_fusion.3
  97.0 0.3 fusion.107
  97.3 2.5 %fusion.84 = f32[256,1024]{1,0:T(8,128)S(1)} fusion(bf16[1024,3072]{1,0:T(8,128)(2,1)} %get-tuple-element.142, bf16[512,1024]{1,0:T(8,128)(2,1)} %get-tuple-element.144), kind=kOutput, calls=%fused_computation.114 | convolution fusion | flops 536870912 | bytes 3670016 | tf_op jit(solution)/shard_map/cond/branch_3_fun/dot_general | solution.py:23
  99.9 2.5 %fusion.86 = f32[256,1024]{1,0:T(8,128)S(1)} fusion(bf16[1024,3072]{1,0:T(8,128)(2,1)} %get-tuple-element.142, bf16[512,1024]{1,0:T(8,128)(2,1)} %get-tuple-element.143), kind=kOutput, calls=%fused_computation.116 | convolution fusion | flops 536870912 | bytes 3670016 | tf_op jit(solution)/shard_map/cond/branch_3_fun/dot_general | solution.py:23
  102.4 0.2 broadcast_select_fusion.19
  102.6 2.8 %fusion.171 = (f32[256]{0:T(256)S(1)}, f32[256]{0:T(256)S(1)}, f32[256,1024]{1,0:T(8,128)S(1)}) fusion(f32[256]{0:T(256)S(1)} %add_rsqrt_fusion.3, f32[256]{0:T(256)S(1)} %broadcast_multiply_fusion.11, bf16[256,1024]{1,0:T(8,128)(2,1)S(1)} %get-tuple-element.140, f32[1024]{0:T(1024)S(1)} %get-tuple-element.145, f32[256,1024]{1,0:T(8,128)S(1)} %fusion.84, ...), kind=kOutput, calls=%fused_computation.241 | convolution fusion | flops 539229696 | bytes 6299648 | tf_op jit(solution)/shard_map/cond/branch_3_fun/dot_general | solution.py:23
  105.3 1.0 pad_maximum_fusion.6
  106.4 0.3 fusion.106
  106.7 6.3 %collective-permute-done.3 = bf16[256,1024]{1,0:T(8,128)(2,1)S(1)} collective-permute-done((bf16[256,1024]{1,0:T(8,128)(2,1)S(1)}, bf16[256,1024]{1,0:T(8,128)(2,1)S(1)}, u32[]{:S(2)}, u32[]{:S(2)}) %collective-permute-start.3) | collective-permute-done | bytes 524320 | tf_op jit(solution)/shard_map/cond/branch_3_fun/ppermute | solution.py:19
  113.0 0.1 broadcast_select_fusion.17
  113.1 1.0 pad_maximum_fusion.7
  (40 shorter events, 0.3 us)
Async XLA Ops:
  0.6 8.8 %copy-start.4 = (bf16[512,1024]{1,0:T(8,128)(2,1)S(1)}, bf16[512,1024]{1,0:T(8,128)(2,1)}, u32[]{:S(2)}) copy-start(bf16[512,1024]{1,0:T(8,128)(2,1)} %param.14) | copy-start | bytes 3145732
  0.6 10.5 %collective-permute-start.5 = (bf16[512,3072]{1,0:T(8,128)(2,1)}, bf16[512,3072]{1,0:T(8,128)(2,1)}, u32[]{:S(2)}, u32[]{:S(2)}) collective-permute-start(bf16[512,3072]{1,0:T(8,128)(2,1)} %param.13), channel_id=1, source_target_pairs={{0,1},{1,0},{2,3},{3,2},{4,5},{5,4},{6,7},{7,6},{8,9},{9,8},{10,11... | collective-permute-start | bytes 9437192 | tf_op jit(solution)/shard_map/ppermute | solution.py:178
  1.2 8.2 %collective-permute-start.6 = (bf16[512,1024]{1,0:T(8,128)(2,1)}, bf16[512,1024]{1,0:T(8,128)(2,1)S(1)}, u32[]{:S(2)}, u32[]{:S(2)}) collective-permute-start(bf16[512,1024]{1,0:T(8,128)(2,1)} %param.14), channel_id=1, source_target_pairs={{0,1},{1,0},{2,3},{3,2},{4,5},{5,4},{6,7},{7,6},{8,9},{9,8},{10,11... | collective-permute-start | bytes 3145736 | tf_op jit(solution)/shard_map/ppermute | solution.py:180
  3.8 27.6 %collective-permute-start.4 = (bf16[256,1024]{1,0:T(8,128)(2,1)}, bf16[256,1024]{1,0:T(8,128)(2,1)S(1)}, u32[]{:S(2)}, u32[]{:S(2)}) collective-permute-start(bf16[256,1024]{1,0:T(8,128)(2,1)} %constant_dynamic-slice_fusion.5), channel_id=1, source_target_pairs={{0,8},{2,10},{4,12},{6,14},{8,0},{10,2},{12,4},{14,6},{1,9},{3,11}... | collective-permute-start | bytes 1572872 | tf_op jit(solution)/shard_map/ppermute | solution.py:19
  7.8 1.8 %copy-start.10 = (bf16[1,1,8,8,8,1024]{5,4,3,2,1,0:T(8,128)(2,1)S(1)}, bf16[1,1,8,8,8,1024]{5,4,3,2,1,0:T(8,128)(2,1)}, u32[]{:S(2)}) copy-start(bf16[1,1,8,8,8,1024]{5,4,3,2,1,0:T(8,128)(2,1)} %param.11) | copy-start | bytes 3145732
  9.6 5.2 %copy-start.5 = (bf16[512,1024]{1,0:T(8,128)(2,1)}, bf16[512,1024]{1,0:T(8,128)(2,1)S(1)}, u32[]{:S(2)}) copy-start(bf16[512,1024]{1,0:T(8,128)(2,1)S(1)} %get-tuple-element.271) | copy-start | bytes 3145732
  9.6 5.2 %copy-start.7 = (bf16[512,1024]{1,0:T(8,128)(2,1)}, bf16[512,1024]{1,0:T(8,128)(2,1)S(1)}, u32[]{:S(2)}) copy-start(bf16[512,1024]{1,0:T(8,128)(2,1)S(1)} %get-tuple-element.272) | copy-start | bytes 3145732
  9.6 2.8 %copy-start.2 = (bf16[512,3072]{1,0:T(8,128)(2,1)S(1)}, bf16[512,3072]{1,0:T(8,128)(2,1)}, u32[]{:S(2)}) copy-start(bf16[512,3072]{1,0:T(8,128)(2,1)} %param.13) | copy-start | bytes 9437188
  11.2 3.6 %copy-start.12 = (f32[1024]{0:T(1024)S(1)}, f32[1024]{0:T(1024)}, u32[]{:S(2)}) copy-start(f32[1024]{0:T(1024)} %param.15) | copy-start | bytes 12292
  14.7 16.6 %copy-start.3 = (bf16[1,1,8,8,8,1024]{5,4,3,2,1,0:T(8,128)(2,1)S(1)}, bf16[1,1,8,8,8,1024]{5,4,3,2,1,0:T(8,128)(2,1)}, u32[]{:S(2)}) copy-start(bf16[1,1,8,8,8,1024]{5,4,3,2,1,0:T(8,128)(2,1)} %param.10) | copy-start | bytes 3145732
  31.7 0.8 copy-start
  35.0 25.6 %collective-permute-start.7 = (bf16[256,1024]{1,0:T(8,128)(2,1)S(1)}, bf16[256,1024]{1,0:T(8,128)(2,1)S(1)}, u32[]{:S(2)}, u32[]{:S(2)}) collective-permute-start(bf16[256,1024]{1,0:T(8,128)(2,1)S(1)} %constant_dynamic-slice_fusion.3), channel_id=1, source_target_pairs={{0,8},{2,10},{4,12},{6,14},{8,0},{10,2},{12,4},{14,6},{1,9},{3,11}... | collective-permute-start | bytes 1572872 | tf_op jit(solution)/shard_map/ppermute | solution.py:19
  50.0 13.7 %copy-start.6 = (bf16[512,1024]{1,0:T(8,128)(2,1)S(1)}, bf16[512,1024]{1,0:T(8,128)(2,1)}, u32[]{:S(2)}) copy-start(bf16[512,1024]{1,0:T(8,128)(2,1)} %copy-done.5) | copy-start | bytes 3145732
  50.0 13.7 %copy-start.8 = (bf16[512,1024]{1,0:T(8,128)(2,1)S(1)}, bf16[512,1024]{1,0:T(8,128)(2,1)}, u32[]{:S(2)}) copy-start(bf16[512,1024]{1,0:T(8,128)(2,1)} %copy-done.7) | copy-start | bytes 3145732
  60.6 0.8 copy-start.13
  63.7 1.2 %copy-start.11 = (bf16[1,1,8,8,8,1024]{5,4,3,2,1,0:T(8,128)(2,1)S(1)}, bf16[1,1,8,8,8,1024]{5,4,3,2,1,0:T(8,128)(2,1)}, u32[]{:S(2)}) copy-start(bf16[1,1,8,8,8,1024]{5,4,3,2,1,0:T(8,128)(2,1)} %param.11) | copy-start | bytes 3145732
  63.7 1.3 %copy-start.14 = (bf16[256,1024]{1,0:T(8,128)(2,1)S(1)}, bf16[256,1024]{1,0:T(8,128)(2,1)}, u32[]{:S(2)}) copy-start(bf16[256,1024]{1,0:T(8,128)(2,1)} %copy-done.13) | copy-start | bytes 1572868
  65.1 1.0 copy-start.9
  65.8 24.6 %collective-permute-start.8 = (bf16[256,1024]{1,0:T(8,128)(2,1)S(1)}, bf16[256,1024]{1,0:T(8,128)(2,1)S(1)}, u32[]{:S(2)}, u32[]{:S(2)}) collective-permute-start(bf16[256,1024]{1,0:T(8,128)(2,1)S(1)} %convolution_convert_fusion.3), channel_id=1, source_target_pairs={{0,8},{2,10},{4,12},{6,14},{8,0},{10,2},{12,4},{14,6},{1,9},{3,11}... | collective-permute-start | bytes 1572872 | tf_op jit(solution)/shard_map/ppermute | solution.py:19
  92.2 1.9 %copy-start.1 = (bf16[256,1024]{1,0:T(8,128)(2,1)S(1)}, bf16[256,1024]{1,0:T(8,128)(2,1)}, u32[]{:S(2)}) copy-start(bf16[256,1024]{1,0:T(8,128)(2,1)} %copy-done) | copy-start | bytes 1572868
  96.8 16.2 %collective-permute-start.3 = (bf16[256,1024]{1,0:T(8,128)(2,1)S(1)}, bf16[256,1024]{1,0:T(8,128)(2,1)S(1)}, u32[]{:S(2)}, u32[]{:S(2)}) collective-permute-start(bf16[256,1024]{1,0:T(8,128)(2,1)S(1)} %get-tuple-element.146), channel_id=1, source_target_pairs={{0,8},{2,10},{4,12},{6,14},{8,0},{10,2},{12,4},{14,6},{1,9},{3,11}... | collective-permute-start | bytes 1572872 | tf_op jit(solution)/shard_map/cond/branch_3_fun/ppermute | solution.py:19
